TPU v7x, 32 devices: a whole 2x2x4 slice. The times are simulated.
32 devices in a mesh: groups: 2 (over x), acq: 16 (over z, y, core).
Axes of the slice: x: 2, y: 2, z: 4, core: 2. Of those that a mesh axis runs over, the one named last changes fastest.
Arguments:
- measurements: bfloat16 [128, 2, 16, 12, 256], P(('groups', 'acq')), parts along dimension 0, may hold values from -96 to 96
- tile_order: int32 [32], P('groups'), parts along dimension 0, may hold values from 0 to 15, each once
- steer_phase: float32 [32, 64, 512], P(('groups', 'acq')), parts along dimension 0, may hold values from -3.140625 to 3.140625
- group_ids: int32 [384, 256], P(('groups', 'acq')), parts along dimension 0, may hold values from 0 to 49151, as said below
Outputs:
- elevation_profile: bfloat16 [384, 256, 1024], P(('groups', 'acq')), parts along dimension 0
There are 2 independent parts, one for each index of `groups`. A program takes and returns all parts, laid end to end along the dimension named above; each array names one. Nothing has to cross between parts.
Inputs may be any that keep to these rules, and one draw needn't show every extreme that they name: `tile_order`: each tile of the window appears once. `group_ids`: equal labels mark the pixels of one joint group; the window's rows fall into bands of 3 consecutive rows (fewer at its top, and a band begins at its last row), each band's columns into runs of 3 consecutive columns (fewer at its sides; in the last band a run begins at the last column), and each band-run rectangle is one group; a group's label is the flat index row * 256 + column of its top-left pixel.
All inputs are finite; a program needn't handle non-finite values.
Results may differ from a plain program's by a relative error of at most 0.0054.
Values may be sent and summed in bfloat16 or wider, within the bound.
No kernel may reach another device: no remote copies, remote signals or barrier semaphores. Data moves between devices by JAX's collectives and lax.ppermute only.
A program may use at most 128 MiB of HBM per device.

v0:
```python
import math

import jax
import jax.numpy as jnp
from jax import lax
from jax.sharding import PartitionSpec as P

ITERS = 3


STEP_SIZE = 0.0625
SHRINK_LEVEL = 3.0


def padded_2(cells, sides, width):
    for axis, dim in sides:
        count = lax.axis_size(axis)
        ends = count - 1
        head = lax.slice_in_dim(cells, 0, width, axis=dim)
        tail = lax.slice_in_dim(cells, cells.shape[dim] - width, cells.shape[dim], axis=dim)
        cells = jnp.concatenate(
            [
                lax.ppermute(tail, axis, [(i, (i + 1) % count) for i in range(ends)]),
                cells,
                lax.ppermute(head, axis, [((i + 1) % count, i) for i in range(ends)]),
            ],
            axis=dim,
        )
    return cells


def row_pass(energy, labels):
    columns = labels.shape[1]
    padded = jnp.pad(energy, ((0, 0), (2, 2), (0, 0)))
    padded_ids = jnp.pad(labels, ((0, 0), (2, 2)), constant_values=-1)
    accumulated = jnp.zeros(energy.shape, jnp.float32)
    for offset in range(5):
        same = padded_ids[:, offset : offset + columns] == labels
        accumulated = accumulated + jnp.where(
            same[:, :, None], padded[:, offset : offset + columns], 0.0
        )
    return accumulated


def column_pass(stacked, labels_ext, row_count):
    accumulated = jnp.zeros((row_count,) + stacked.shape[1:], jnp.float32)
    for offset in range(5):
        same = labels_ext[offset : offset + row_count] == labels_ext[2 : 2 + row_count]
        accumulated = accumulated + jnp.where(
            same[:, :, None], stacked[offset : offset + row_count], 0.0
        )
    return accumulated


def energy_of(stepped, row_count, columns, elevations):
    energy = (
        stepped[:, :elevations] * stepped[:, :elevations]
        + stepped[:, elevations:] * stepped[:, elevations:]
    )
    return energy.reshape(row_count, columns, elevations)


def build_steering(phase, acquisitions, elevations):
    norm_scale = 1.0 / math.sqrt(acquisitions)
    real_part = (jnp.cos(phase) * norm_scale).astype(jnp.bfloat16)
    imag_part = (jnp.sin(phase) * norm_scale).astype(jnp.bfloat16)
    upper_block = jnp.concatenate([real_part.T, -imag_part.T], axis=0)
    lower_block = jnp.concatenate([imag_part.T, real_part.T], axis=0)
    return jnp.stack([upper_block, lower_block], axis=2).reshape(2 * elevations, 2 * acquisitions)


def update(steering, iter_rows, target_rows, is_first):
    if is_first:
        residual = -target_rows.astype(jnp.float32)
    else:
        predicted = lax.dot_general(
            steering,
            iter_rows.astype(jnp.bfloat16),
            (((0,), (1,)), ((), ())),
            preferred_element_type=jnp.float32,
        )
        residual = predicted - target_rows.astype(jnp.float32)
    gradient = lax.dot_general(
        residual.astype(jnp.bfloat16),
        steering,
        (((0,), (1,)), ((), ())),
        preferred_element_type=jnp.float32,
    )
    return iter_rows - STEP_SIZE * gradient


def on_device(measurements, tile_order, steer_phase, group_ids):
    tile_count = tile_order.shape[0]
    places = (
        jnp.zeros((tile_count,), jnp.int32)
        .at[tile_order]
        .set(jnp.arange(tile_count, dtype=jnp.int32))
    )
    ordered = jnp.take(measurements, places, axis=2)
    gathered = lax.all_to_all(ordered, "acq", split_axis=2, concat_axis=0, tiled=True)
    acquisitions = gathered.shape[0]
    tile_rows = gathered.shape[3]
    columns = gathered.shape[4]
    pixels = tile_rows * columns
    elevations = steer_phase.shape[2]
    depth = 2 * ITERS
    labels_deep = padded_2(group_ids, (("acq", 0),), 2 * ITERS)
    labels_ext = labels_deep[depth - 2 : depth + tile_rows + 2]
    edge_labels = jnp.concatenate([labels_ext[:2], labels_ext[-2:]], axis=0)
    targets = gathered.reshape(2 * acquisitions, pixels)
    steering = build_steering(steer_phase[0], acquisitions, elevations)
    iterate = jnp.zeros((pixels, 2 * elevations), jnp.float32)
    for iteration in range(ITERS):
        is_first = iteration == 0
        stepped = update(steering, iterate, targets, is_first)
        row_count = group_ids.shape[0]
        payload = energy_of(stepped, row_count, columns, elevations)
        extended = padded_2(payload.astype(jnp.bfloat16), (("acq", 0),), 2).astype(payload.dtype)
        near_rows = jnp.concatenate([extended[:2], extended[-2:]], axis=0)
        near_sums = row_pass(near_rows, edge_labels)
        local_sums = row_pass(energy_of(stepped, tile_rows, columns, elevations), group_ids)
        stacked = jnp.concatenate([near_sums[:2], local_sums, near_sums[2:]], axis=0)
        group_norm = jnp.sqrt(column_pass(stacked, labels_ext, tile_rows))
        factor = jnp.maximum(group_norm - SHRINK_LEVEL, 0.0) / jnp.maximum(group_norm, SHRINK_LEVEL)
        factor = factor.reshape(pixels, elevations)
        iterate = stepped * jnp.concatenate([factor, factor], axis=1)
    return iterate.reshape(tile_rows, columns, 2 * elevations).astype(jnp.bfloat16)


def solution(mesh):
    placed = (
        P(("groups", "acq"), None, None, None, None),
        P("groups"),
        P(("groups", "acq"), None, None),
        P(("groups", "acq"), None),
    )
    return jax.shard_map(
        on_device,
        mesh=mesh,
        in_specs=placed,
        out_specs=P(("groups", "acq"), None, None),
        check_vma=False,
    )
```

profile of v0, /device:TPU:14, one launch (start us, length us, event | category | flops | bytes accessed | tf_op | source)
XLA Modules:
  0.0 186.6 jit_solution(3563389345103228980)
XLA Ops:
  1.4 2.8 %gather_fusion = bf16[16,4,2,12,256]{4,0,3,2,1:T(8,128)(2,1)S(1)} fusion(bf16[4,2,16,12,256]{4,2,3,1,0:T(8,128)(2,1)S(1)} %copy-done, s32[1024]{0:T(1024)S(1)} %pad_clamp_fusion), kind=kCustom, calls=%fused_computation | custom fusion | bytes 1572928 | tf_op jit(solution)/shard_map/jit(_take)/gather | solution.py:99
  4.4 1.5 copy.10
  5.9 6.2 %all-to-all-start = ((bf16[4,2,16,12,256]{4,0,3,1,2:T(4,128)(2,1)}), bf16[4,2,16,12,256]{4,0,3,1,2:T(4,128)(2,1)S(1)}, u32[]{:S(2)}, u32[]{:S(2)}) async-start(bf16[4,2,16,12,256]{4,0,3,1,2:T(4,128)(2,1)} %copy.10), calls=%async_computation | async-start | bytes 1572864 | tf_op jit(solution)/shard_map/all_to_all | solution.py:100
  12.1 2.0 %collective-permute-start = (s32[6,256]{1,0:T(8,128)S(1)}, s32[6,256]{1,0:T(8,128)S(1)}, u32[]{:S(2)}, u32[]{:S(2)}) collective-permute-start(s32[6,256]{1,0:T(8,128)S(1)} %get-tuple-element.37), channel_id=1, source_target_pairs={{0,1},{1,2},{2,3},{3,4},{4,5},{5,6},{6,7},{7,8},{8,9},{9,10},{10,1... | collective-permute-start | bytes 18440 | tf_op jit(solution)/shard_map/ppermute | solution.py:23
  14.2 3.7 %collective-permute-start.1 = (s32[6,256]{1,0:T(8,128)S(1)}, s32[6,256]{1,0:T(8,128)S(1)}, u32[]{:S(2)}, u32[]{:S(2)}) collective-permute-start(s32[6,256]{1,0:T(8,128)S(1)} %get-tuple-element.38), channel_id=1, source_target_pairs={{1,0},{2,1},{3,2},{4,3},{5,4},{6,5},{7,6},{8,7},{9,8},{10,9},{11,1... | collective-permute-start | bytes 18440 | tf_op jit(solution)/shard_map/ppermute | solution.py:25
  19.5 11.6 %all-to-all-done = bf16[4,2,16,12,256]{4,0,3,1,2:T(4,128)(2,1)S(1)} async-done(((bf16[4,2,16,12,256]{4,0,3,1,2:T(4,128)(2,1)}), bf16[4,2,16,12,256]{4,0,3,1,2:T(4,128)(2,1)S(1)}, u32[]{:S(2)}, u32[]{:S(2)}) %all-to-all-start) | async-done | bytes 786464 | tf_op jit(solution)/shard_map/all_to_all | solution.py:100
  34.1 1.8 multiply_subtract_fusion.2
  36.0 4.9 %fusion.38 = f32[3072,512]{1,0:T(8,128)} fusion(f32[3072,1024]{1,0:T(8,128)S(1)} %multiply_subtract_fusion.2), kind=kLoop, calls=%fused_computation.69 | loop fusion | flops 4718592 | bytes 18874368 | tf_op jit(solution)/shard_map/add | solution.py:57
  40.8 1.6 copy-done.2
  42.4 3.4 %convert_element_type.89 = bf16[12,256,512]{2,1,0:T(8,128)(2,1)S(1)} convert(f32[12,256,512]{2,1,0:T(8,128)} %bitcast.53) | non-fusion elementwise | flops 1572864 | bytes 9437184 | tf_op jit(solution)/shard_map/convert_element_type | solution.py:118
  45.8 2.7 %collective-permute-start.2 = (bf16[2,256,512]{2,1,0:T(8,128)(2,1)S(1)}, bf16[2,256,512]{2,1,0:T(8,128)(2,1)S(1)}, u32[]{:S(2)}, u32[]{:S(2)}) collective-permute-start(bf16[2,256,512]{2,1,0:T(8,128)(2,1)S(1)} %get-tuple-element.17), channel_id=1, source_target_pairs={{0,1},{1,2},{2,3},{3,4},{4,5},{5,6},{6,7},{7,8},{8,9},{9,10},{10,1... | collective-permute-start | bytes 1572872 | tf_op jit(solution)/shard_map/ppermute | solution.py:23
  48.6 3.2 %collective-permute-start.3 = (bf16[2,256,512]{2,1,0:T(8,128)(2,1)S(1)}, bf16[2,256,512]{2,1,0:T(8,128)(2,1)S(1)}, u32[]{:S(2)}, u32[]{:S(2)}) collective-permute-start(bf16[2,256,512]{2,1,0:T(8,128)(2,1)S(1)} %get-tuple-element.18), channel_id=1, source_target_pairs={{1,0},{2,1},{3,2},{4,3},{5,4},{6,5},{7,6},{8,7},{9,8},{10,9},{11,1... | collective-permute-start | bytes 1572872 | tf_op jit(solution)/shard_map/ppermute | solution.py:25
  51.8 4.2 %select_add_fusion.2 = f32[12,256,512]{2,1,0:T(8,128)S(1)} fusion(f32[12,256,512]{2,1,0:T(8,128)S(1)} %bitcast.56, pred[12,256]{1,0:T(8,128)(4,1)S(1)} %get-tuple-element.34, pred[12,256]{1,0:T(8,128)(4,1)S(1)} %get-tuple-element.31, pred[12,256]{1,0:T(8,128)(4,1)S(1)} %get-tuple-element.32, pred[12,256]{1,0:T(8,128)(4,1)S(1)} %get-tuple-element.33), kind=kLoop, calls=%fused_computation.80 | loop fusion | flops 12582912 | bytes 12595200 | tf_op jit(solution)/shard_map/add | solution.py:39
  56.0 6.1 %collective-permute-done.2 = bf16[2,256,512]{2,1,0:T(8,128)(2,1)S(1)} collective-permute-done((bf16[2,256,512]{2,1,0:T(8,128)(2,1)S(1)}, bf16[2,256,512]{2,1,0:T(8,128)(2,1)S(1)}, u32[]{:S(2)}, u32[]{:S(2)}) %collective-permute-start.2) | collective-permute-done | bytes 524320 | tf_op jit(solution)/shard_map/ppermute | solution.py:23
  62.4 1.4 select_add_fusion.5
  64.0 6.8 %maximum_divide_fusion.2 = f32[12,256,512]{2,1,0:T(8,128)} fusion(f32[2,256,512]{2,1,0:T(8,128)S(1)} %get-tuple-element.24, f32[12,256,512]{2,1,0:T(8,128)S(1)} %select_add_fusion.2, f32[2,256,512]{2,1,0:T(8,128)S(1)} %get-tuple-element.23, pred[12,256]{1,0:T(8,128)(4,1)S(1)} %get-tuple-element.35, pred[12,256]{1,0:T(8,128)(4,1)S(1)} %get-tuple-element.36, ...), kind=kLoop, calls=%fused_computation.79 | loop fusion | flops 25165824 | bytes 14692352 | tf_op jit(solution)/shard_map/div | solution.py:124
  70.8 24.7 %multiply_subtract_fusion.1 = f32[3072,1024]{1,0:T(8,128)} fusion(bf16[1024,128]{0,1:T(8,128)(2,1)S(1)} %reshape.61, f32[3072,1024]{1,0:T(8,128)} %copy-done.2, f32[3072,512]{1,0:T(8,128)} %bitcast.50, f32[128,3072]{1,0:T(8,128)S(1)} %bitcast.60), kind=kOutput, calls=%fused_computation.7 | convolution fusion | flops 1633419264 | bytes 33292288 | tf_op jit(solution)/shard_map/dot_general | solution.py:83
  95.5 6.2 %fusion.35 = f32[3072,512]{1,0:T(8,128)S(1)} fusion(f32[3072,1024]{1,0:T(8,128)} %multiply_subtract_fusion.1), kind=kLoop, calls=%fused_computation.62 | loop fusion | flops 4718592 | bytes 18874368 | tf_op jit(solution)/shard_map/add | solution.py:57
  102.2 1.9 %collective-permute-start.4 = (bf16[2,256,512]{2,1,0:T(8,128)(2,1)S(1)}, bf16[2,256,512]{2,1,0:T(8,128)(2,1)S(1)}, u32[]{:S(2)}, u32[]{:S(2)}) collective-permute-start(bf16[2,256,512]{2,1,0:T(8,128)(2,1)S(1)} %get-tuple-element.15), channel_id=1, source_target_pairs={{0,1},{1,2},{2,3},{3,4},{4,5},{5,6},{6,7},{7,8},{8,9},{9,10},{10,1... | collective-permute-start | bytes 1572872 | tf_op jit(solution)/shard_map/ppermute | solution.py:23
  104.1 3.6 %collective-permute-start.5 = (bf16[2,256,512]{2,1,0:T(8,128)(2,1)S(1)}, bf16[2,256,512]{2,1,0:T(8,128)(2,1)S(1)}, u32[]{:S(2)}, u32[]{:S(2)}) collective-permute-start(bf16[2,256,512]{2,1,0:T(8,128)(2,1)S(1)} %get-tuple-element.16), channel_id=1, source_target_pairs={{1,0},{2,1},{3,2},{4,3},{5,4},{6,5},{7,6},{8,7},{9,8},{10,9},{11,1... | collective-permute-start | bytes 1572872 | tf_op jit(solution)/shard_map/ppermute | solution.py:25
  107.8 4.2 %select_add_fusion.1 = f32[12,256,512]{2,1,0:T(8,128)S(1)} fusion(f32[12,256,512]{2,1,0:T(8,128)S(1)} %bitcast.58, pred[12,256]{1,0:T(8,128)(4,1)S(1)} %get-tuple-element.34, pred[12,256]{1,0:T(8,128)(4,1)S(1)} %get-tuple-element.31, pred[12,256]{1,0:T(8,128)(4,1)S(1)} %get-tuple-element.32, pred[12,256]{1,0:T(8,128)(4,1)S(1)} %get-tuple-element.33), kind=kLoop, calls=%fused_computation.76 | loop fusion | flops 12582912 | bytes 12595200 | tf_op jit(solution)/shard_map/add | solution.py:39
  112.0 6.4 %collective-permute-done.4 = bf16[2,256,512]{2,1,0:T(8,128)(2,1)S(1)} collective-permute-done((bf16[2,256,512]{2,1,0:T(8,128)(2,1)S(1)}, bf16[2,256,512]{2,1,0:T(8,128)(2,1)S(1)}, u32[]{:S(2)}, u32[]{:S(2)}) %collective-permute-start.4) | collective-permute-done | bytes 524320 | tf_op jit(solution)/shard_map/ppermute | solution.py:23
  118.7 1.4 select_add_fusion.4
  120.2 6.8 %maximum_divide_fusion.1 = f32[12,256,512]{2,1,0:T(8,128)} fusion(f32[2,256,512]{2,1,0:T(8,128)S(1)} %get-tuple-element.22, f32[12,256,512]{2,1,0:T(8,128)S(1)} %select_add_fusion.1, f32[2,256,512]{2,1,0:T(8,128)S(1)} %get-tuple-element.21, pred[12,256]{1,0:T(8,128)(4,1)S(1)} %get-tuple-element.35, pred[12,256]{1,0:T(8,128)(4,1)S(1)} %get-tuple-element.36, ...), kind=kLoop, calls=%fused_computation.75 | loop fusion | flops 25165824 | bytes 14692352 | tf_op jit(solution)/shard_map/div | solution.py:124
  127.0 24.8 %multiply_subtract_fusion = f32[3072,1024]{1,0:T(8,128)} fusion(bf16[1024,128]{0,1:T(8,128)(2,1)S(1)} %reshape.61, f32[3072,1024]{1,0:T(8,128)} %multiply_subtract_fusion.1, f32[3072,512]{1,0:T(8,128)} %bitcast.49, f32[128,3072]{1,0:T(8,128)S(1)} %bitcast.61), kind=kOutput, calls=%fused_computation.6 | convolution fusion | flops 1633419264 | bytes 33292288 | tf_op jit(solution)/shard_map/dot_general | solution.py:83
  151.8 6.2 %fusion.32 = f32[3072,512]{1,0:T(8,128)S(1)} fusion(f32[3072,1024]{1,0:T(8,128)} %multiply_subtract_fusion), kind=kLoop, calls=%fused_computation.55 | loop fusion | flops 4718592 | bytes 18874368 | tf_op jit(solution)/shard_map/add | solution.py:57
  158.5 1.9 %collective-permute-start.6 = (bf16[2,256,512]{2,1,0:T(8,128)(2,1)S(1)}, bf16[2,256,512]{2,1,0:T(8,128)(2,1)S(1)}, u32[]{:S(2)}, u32[]{:S(2)}) collective-permute-start(bf16[2,256,512]{2,1,0:T(8,128)(2,1)S(1)} %get-tuple-element.13), channel_id=1, source_target_pairs={{0,1},{1,2},{2,3},{3,4},{4,5},{5,6},{6,7},{7,8},{8,9},{9,10},{10,1... | collective-permute-start | bytes 1572872 | tf_op jit(solution)/shard_map/ppermute | solution.py:23
  160.5 3.6 %collective-permute-start.7 = (bf16[2,256,512]{2,1,0:T(8,128)(2,1)S(1)}, bf16[2,256,512]{2,1,0:T(8,128)(2,1)S(1)}, u32[]{:S(2)}, u32[]{:S(2)}) collective-permute-start(bf16[2,256,512]{2,1,0:T(8,128)(2,1)S(1)} %get-tuple-element.14), channel_id=1, source_target_pairs={{1,0},{2,1},{3,2},{4,3},{5,4},{6,5},{7,6},{8,7},{9,8},{10,9},{11,1... | collective-permute-start | bytes 1572872 | tf_op jit(solution)/shard_map/ppermute | solution.py:25
  164.1 4.2 %select_add_fusion = f32[12,256,512]{2,1,0:T(8,128)S(1)} fusion(f32[12,256,512]{2,1,0:T(8,128)S(1)} %bitcast.52, pred[12,256]{1,0:T(8,128)(4,1)S(1)} %get-tuple-element.34, pred[12,256]{1,0:T(8,128)(4,1)S(1)} %get-tuple-element.31, pred[12,256]{1,0:T(8,128)(4,1)S(1)} %get-tuple-element.32, pred[12,256]{1,0:T(8,128)(4,1)S(1)} %get-tuple-element.33), kind=kLoop, calls=%fused_computation.72 | loop fusion | flops 12582912 | bytes 12595200 | tf_op jit(solution)/shard_map/add | solution.py:39
  168.3 6.4 %collective-permute-done.6 = bf16[2,256,512]{2,1,0:T(8,128)(2,1)S(1)} collective-permute-done((bf16[2,256,512]{2,1,0:T(8,128)(2,1)S(1)}, bf16[2,256,512]{2,1,0:T(8,128)(2,1)S(1)}, u32[]{:S(2)}, u32[]{:S(2)}) %collective-permute-start.6) | collective-permute-done | bytes 524320 | tf_op jit(solution)/shard_map/ppermute | solution.py:23
  176.6 5.8 %maximum_divide_fusion = f32[12,256,512]{2,1,0:T(8,128)S(1)} fusion(f32[2,256,512]{2,1,0:T(8,128)S(1)} %get-tuple-element.20, f32[12,256,512]{2,1,0:T(8,128)S(1)} %select_add_fusion, f32[2,256,512]{2,1,0:T(8,128)S(1)} %get-tuple-element.19, pred[12,256]{1,0:T(8,128)(4,1)S(1)} %get-tuple-element.35, pred[12,256]{1,0:T(8,128)(4,1)S(1)} %get-tuple-element.36, ...), kind=kLoop, calls=%fused_computation.71 | loop fusion | flops 25165824 | bytes 14692352 | tf_op jit(solution)/shard_map/div | solution.py:124
  182.5 4.1 %fusion = bf16[3072,1024]{1,0:T(8,128)(2,1)} fusion(f32[3072,1024]{1,0:T(8,128)S(1)} %bitcast.48, f32[3072,512]{1,0:T(8,128)S(1)} %bitcast.59), kind=kLoop, calls=%fused_computation.5 | loop fusion | flops 9437184 | bytes 25165824 | tf_op jit(solution)/shard_map/convert_element_type | solution.py:127
  (66 shorter events, 10.0 us)
Async XLA Ops:
  0.0 1.4 copy-start
  1.4 10.7 %copy-start.4 = (s32[12,256]{1,0:T(8,128)S(1)}, s32[12,256]{1,0:T(8,128)}, u32[]{:S(2)}) copy-start(s32[12,256]{1,0:T(8,128)} %param.7) | copy-start | bytes 36868
  1.4 16.5 %copy-start.3 = (f32[1,64,512]{2,1,0:T(8,128)S(1)}, f32[1,64,512]{2,1,0:T(8,128)}, u32[]{:S(2)}) copy-start(f32[1,64,512]{2,1,0:T(8,128)} %param.6) | copy-start | bytes 393220
  5.9 25.2 %all-to-all-start = ((bf16[4,2,16,12,256]{4,0,3,1,2:T(4,128)(2,1)}), bf16[4,2,16,12,256]{4,0,3,1,2:T(4,128)(2,1)S(1)}, u32[]{:S(2)}, u32[]{:S(2)}) async-start(bf16[4,2,16,12,256]{4,0,3,1,2:T(4,128)(2,1)} %copy.10), calls=%async_computation | async-start | bytes 1572864 | tf_op jit(solution)/shard_map/all_to_all | solution.py:100
  12.1 7.1 %collective-permute-start = (s32[6,256]{1,0:T(8,128)S(1)}, s32[6,256]{1,0:T(8,128)S(1)}, u32[]{:S(2)}, u32[]{:S(2)}) collective-permute-start(s32[6,256]{1,0:T(8,128)S(1)} %get-tuple-element.37), channel_id=1, source_target_pairs={{0,1},{1,2},{2,3},{3,4},{4,5},{5,6},{6,7},{7,8},{8,9},{9,10},{10,1... | collective-permute-start | bytes 18440 | tf_op jit(solution)/shard_map/ppermute | solution.py:23
  14.2 5.1 %collective-permute-start.1 = (s32[6,256]{1,0:T(8,128)S(1)}, s32[6,256]{1,0:T(8,128)S(1)}, u32[]{:S(2)}, u32[]{:S(2)}) collective-permute-start(s32[6,256]{1,0:T(8,128)S(1)} %get-tuple-element.38), channel_id=1, source_target_pairs={{1,0},{2,1},{3,2},{4,3},{5,4},{6,5},{7,6},{8,7},{9,8},{10,9},{11,1... | collective-permute-start | bytes 18440 | tf_op jit(solution)/shard_map/ppermute | solution.py:25
  35.9 6.4 %copy-start.2 = (f32[3072,1024]{1,0:T(8,128)}, f32[3072,1024]{1,0:T(8,128)S(1)}, u32[]{:S(2)}) copy-start(f32[3072,1024]{1,0:T(8,128)S(1)} %multiply_subtract_fusion.2) | copy-start | bytes 37748740
  42.4 9.4 %slice-start.3 = ((s8[6291456]{0:T(1024)(128)(4,1)}), s8[4194304]{0:T(1024)(128)(4,1)S(1)}, s32[]{:S(2)}) async-start(s8[6291456]{0:T(1024)(128)(4,1)} %bitcast.54), calls=%async_computation.4 | async-start | bytes 8388608
  42.4 9.4 %slice-start.4 = ((s8[6291456]{0:T(1024)(128)(4,1)}), s8[2097152]{0:T(1024)(128)(4,1)S(1)}, s32[]{:S(2)}) async-start(s8[6291456]{0:T(1024)(128)(4,1)} %bitcast.54), calls=%async_computation.5 | async-start | bytes 4194304
  45.8 16.2 %collective-permute-start.2 = (bf16[2,256,512]{2,1,0:T(8,128)(2,1)S(1)}, bf16[2,256,512]{2,1,0:T(8,128)(2,1)S(1)}, u32[]{:S(2)}, u32[]{:S(2)}) collective-permute-start(bf16[2,256,512]{2,1,0:T(8,128)(2,1)S(1)} %get-tuple-element.17), channel_id=1, source_target_pairs={{0,1},{1,2},{2,3},{3,4},{4,5},{5,6},{6,7},{7,8},{8,9},{9,10},{10,1... | collective-permute-start | bytes 1572872 | tf_op jit(solution)/shard_map/ppermute | solution.py:23
  48.6 13.5 %collective-permute-start.3 = (bf16[2,256,512]{2,1,0:T(8,128)(2,1)S(1)}, bf16[2,256,512]{2,1,0:T(8,128)(2,1)S(1)}, u32[]{:S(2)}, u32[]{:S(2)}) collective-permute-start(bf16[2,256,512]{2,1,0:T(8,128)(2,1)S(1)} %get-tuple-element.18), channel_id=1, source_target_pairs={{1,0},{2,1},{3,2},{4,3},{5,4},{6,5},{7,6},{8,7},{9,8},{10,9},{11,1... | collective-permute-start | bytes 1572872 | tf_op jit(solution)/shard_map/ppermute | solution.py:25
  102.2 16.1 %collective-permute-start.4 = (bf16[2,256,512]{2,1,0:T(8,128)(2,1)S(1)}, bf16[2,256,512]{2,1,0:T(8,128)(2,1)S(1)}, u32[]{:S(2)}, u32[]{:S(2)}) collective-permute-start(bf16[2,256,512]{2,1,0:T(8,128)(2,1)S(1)} %get-tuple-element.15), channel_id=1, source_target_pairs={{0,1},{1,2},{2,3},{3,4},{4,5},{5,6},{6,7},{7,8},{8,9},{9,10},{10,1... | collective-permute-start | bytes 1572872 | tf_op jit(solution)/shard_map/ppermute | solution.py:23
  104.1 14.2 %collective-permute-start.5 = (bf16[2,256,512]{2,1,0:T(8,128)(2,1)S(1)}, bf16[2,256,512]{2,1,0:T(8,128)(2,1)S(1)}, u32[]{:S(2)}, u32[]{:S(2)}) collective-permute-start(bf16[2,256,512]{2,1,0:T(8,128)(2,1)S(1)} %get-tuple-element.16), channel_id=1, source_target_pairs={{1,0},{2,1},{3,2},{4,3},{5,4},{6,5},{7,6},{8,7},{9,8},{10,9},{11,1... | collective-permute-start | bytes 1572872 | tf_op jit(solution)/shard_map/ppermute | solution.py:25
  158.5 16.1 %collective-permute-start.6 = (bf16[2,256,512]{2,1,0:T(8,128)(2,1)S(1)}, bf16[2,256,512]{2,1,0:T(8,128)(2,1)S(1)}, u32[]{:S(2)}, u32[]{:S(2)}) collective-permute-start(bf16[2,256,512]{2,1,0:T(8,128)(2,1)S(1)} %get-tuple-element.13), channel_id=1, source_target_pairs={{0,1},{1,2},{2,3},{3,4},{4,5},{5,6},{6,7},{7,8},{8,9},{9,10},{10,1... | collective-permute-start | bytes 1572872 | tf_op jit(solution)/shard_map/ppermute | solution.py:23
  160.5 14.2 %collective-permute-start.7 = (bf16[2,256,512]{2,1,0:T(8,128)(2,1)S(1)}, bf16[2,256,512]{2,1,0:T(8,128)(2,1)S(1)}, u32[]{:S(2)}, u32[]{:S(2)}) collective-permute-start(bf16[2,256,512]{2,1,0:T(8,128)(2,1)S(1)} %get-tuple-element.14), channel_id=1, source_target_pairs={{1,0},{2,1},{3,2},{4,3},{5,4},{6,5},{7,6},{8,7},{9,8},{10,9},{11,1... | collective-permute-start | bytes 1572872 | tf_op jit(solution)/shard_map/ppermute | solution.py:25
  175.0 7.5 %slice-start = ((s8[12582912]{0:T(1024)(128)(4,1)}), s8[4194304]{0:T(1024)(128)(4,1)S(1)}, s32[]{:S(2)}) async-start(s8[12582912]{0:T(1024)(128)(4,1)} %bitcast.47), calls=%async_computation.1 | async-start | bytes 8388608
  176.4 6.1 %slice-start.1 = ((s8[12582912]{0:T(1024)(128)(4,1)}), s8[4194304]{0:T(1024)(128)(4,1)S(1)}, s32[]{:S(2)}) async-start(s8[12582912]{0:T(1024)(128)(4,1)} %bitcast.47), calls=%async_computation.2 | async-start | bytes 8388608
  176.6 5.9 %slice-start.2 = ((s8[12582912]{0:T(1024)(128)(4,1)}), s8[4194304]{0:T(1024)(128)(4,1)S(1)}, s32[]{:S(2)}) async-start(s8[12582912]{0:T(1024)(128)(4,1)} %bitcast.47), calls=%async_computation.3 | async-start | bytes 8388608
  182.5 4.1 %copy-start.1 = (bf16[4,2,16,12,256]{4,2,3,1,0:T(8,128)(2,1)S(1)}, bf16[4,2,16,12,256]{4,2,3,1,0:T(8,128)(2,1)}, u32[]{:S(2)}) copy-start(bf16[4,2,16,12,256]{4,2,3,1,0:T(8,128)(2,1)} %param.4) | copy-start | bytes 2359300
where the time goes:
time: 187 us
  other arithmetic  65.5 us (35%)
  matrix products  51.3 us (27%)
  waiting for transfers between devices  30.4 us (16%)
  starting transfers between devices  29 us (16%)
  local copies, waits for them, and re-layouts  9.76 us (5%)
    dot_general x3, matrix products, update(): lax.dot_general(residual.astype(jnp.bfloat16), steering, (((0,), (1,)), (...  51.3 us
    div x3, other arithmetic, on_device(): jnp.maximum(group_norm - SHRINK_LEVEL, 0.0)  19.4 us
    ppermute x4, waiting for transfers between devices, padded_2(): lax.ppermute(tail, axis, [(i, (i + 1) % count) for i in range(ends)])  18.8 us
    add x3, other arithmetic, energy_of(): stepped[:, :elevations] * stepped[:, :elevations]  17.2 us
    add x6, other arithmetic, row_pass(): accumulated + jnp.where(same[:, :, None], padded[:, offset:offset + colum...  16.7 us
    ppermute x4, starting transfers between devices, padded_2(): lax.ppermute(head, axis, [((i + 1) % count, i) for i in range(ends)])  14.2 us
    all_to_all x1, waiting for transfers between devices, on_device(): lax.all_to_all(ordered, 'acq', split_axis=2, concat_axis=0, tiled=True)  11.6 us
    ppermute x4, starting transfers between devices, padded_2(): lax.ppermute(tail, axis, [(i, (i + 1) % count) for i in range(ends)])  8.6 us
  transfers between devices with their start and end apart: 9, of which 4 were waited for; matrix products, arithmetic and copies ran while one was open for 8% of the time, Pallas kernels for 0%

commit v1 on v0

v1 whole, which is shorter than its diff:
```python
import functools
import math

import jax
import jax.numpy as jnp
from jax import lax
from jax.experimental import pallas as pl
from jax.experimental.pallas import tpu as pltpu
from jax.sharding import PartitionSpec as P

ITERS = 3
BAND = 3
STEP_SIZE = 0.0625
SHRINK_LEVEL = 3.0


def dot(a, b, dims=((1,), (0,))):
    return lax.dot_general(a, b, (dims, ((), ())), preferred_element_type=jnp.float32)


def order_kernel(order_ref, stack_ref, sent_ref):
    acqs, parts, rows, tiles, columns = stack_ref.shape
    lines = acqs * parts * tiles
    share = acqs * parts
    target = lax.broadcasted_iota(jnp.int32, (lines, lines), 0)
    source = lax.broadcasted_iota(jnp.int32, (lines, lines), 1)
    block = lax.rem(source, tiles)
    part = lax.rem(lax.div(source, tiles), parts)
    acq = lax.div(source, tiles * parts)
    tile = jnp.zeros((lines, lines), jnp.int32)
    for k in range(tiles):
        tile = jnp.where(block == k, order_ref[k], tile)
    place = tile * share + part * acqs + acq
    pick = jnp.where(target == place, 1.0, 0.0).astype(jnp.bfloat16)
    for row in range(rows):
        lump = stack_ref[:, :, row].reshape(lines, columns)
        sent_ref[:, row * columns : (row + 1) * columns] = dot(pick, lump).astype(sent_ref.dtype)


def order_tiles(measurements, tile_order):
    acqs, parts, tiles, rows, columns = measurements.shape
    stack = measurements.transpose(0, 1, 3, 2, 4)
    chunk = BAND
    return pl.pallas_call(
        order_kernel,
        grid=(rows // chunk,),
        in_specs=[
            pl.BlockSpec(memory_space=pltpu.SMEM),
            pl.BlockSpec((acqs, parts, chunk, tiles, columns), lambda i: (0, 0, i, 0, 0)),
        ],
        out_specs=pl.BlockSpec((acqs * parts * tiles, chunk * columns), lambda i: (0, i)),
        out_shape=jax.ShapeDtypeStruct((acqs * parts * tiles, rows * columns), measurements.dtype),
        name="order_tiles",
    )(tile_order, stack)


def shrink_factor(energy, pick):
    sums = dot(pick, energy.astype(jnp.bfloat16))
    factor = jnp.maximum(1.0 - SHRINK_LEVEL * lax.rsqrt(jnp.maximum(sums, SHRINK_LEVEL**2)), 0.0)
    high = factor.astype(jnp.bfloat16)
    low = (factor - high.astype(jnp.float32)).astype(jnp.bfloat16)
    both = jnp.concatenate([high, low], axis=0)
    return dot(jnp.concatenate([pick, pick], axis=0), both, ((0,), (0,)))


def band_kernel(
    target_ref, run_ref, back_ref, ahead_ref, out_ref,
    target_sc, resid_sc, step_sc, energy_sc, factor_sc, image_sc, sem,
    *, own_rows, tile_width,
):
    band = pl.program_id(0)
    bands = pl.num_programs(0)
    columns = run_ref.shape[2]
    elevations = factor_sc.shape[1]
    groups = -(-(columns // BAND + 2) // 16) * 16
    first = jnp.where(band == 0, 0, 1)
    later = jnp.where(band == bands - 1, 2, 1)
    weight_of = (first,) + (later,) * (BAND - 1)
    span = [slice(q * columns, (q + 1) * columns) for q in range(BAND)]

    def copies(of):
        return [
            (of * BAND + q - 1, pltpu.make_async_copy(
                image_sc.at[q], out_ref.at[jnp.clip(of * BAND + q - 1, 0, own_rows - 1)], sem.at[q]))
            for q in range(BAND)
        ]

    def drain(of):
        for row, copy in copies(of):
            @pl.when(jnp.logical_and(row >= 0, row < own_rows))
            def _(copy=copy):
                copy.wait()

    group = lax.broadcasted_iota(jnp.int32, (groups, columns), 0)
    pick = jnp.where(group == run_ref[0], 1.0, 0.0).astype(jnp.bfloat16)
    target_sc[...] = target_ref[...].astype(jnp.float32).T

    def descend(is_first):
        for at in range(0, elevations, tile_width):
            real = slice(at, at + tile_width)
            imag = slice(elevations + at, elevations + at + tile_width)
            for q in range(BAND):
                if is_first:
                    resid = target_sc[span[q]].astype(jnp.bfloat16)
                else:
                    resid = resid_sc[span[q]]
                step_real = dot(resid, back_ref[weight_of[q], :, real])
                step_imag = dot(resid, back_ref[weight_of[q], :, imag])
                if not is_first:
                    factor = factor_sc[:, real]
                    step_real += step_sc[span[q], real] * factor
                    step_imag += step_sc[span[q], imag] * factor
                step_sc[span[q], real] = step_real
                step_sc[span[q], imag] = step_imag
                energy = step_real * step_real + step_imag * step_imag
                if q > 0:
                    energy += energy_sc[...]
                if q < BAND - 1:
                    energy_sc[...] = energy
            factor_sc[:, real] = shrink_factor(energy, pick)

    def predict():
        for q in range(BAND):
            guess = jnp.zeros((columns, target_sc.shape[1]), jnp.float32)
            for half in range(2):
                part = slice(half * elevations, (half + 1) * elevations)
                rounded = (step_sc[span[q], part] * factor_sc[...]).astype(jnp.bfloat16)
                guess += dot(rounded, ahead_ref[weight_of[q], part])
            resid_sc[span[q]] = (target_sc[span[q]] - guess).astype(jnp.bfloat16)

    descend(True)

    @pl.loop(1, ITERS)
    def _(i):
        predict()
        descend(False)

    @pl.when(band > 0)
    def _():
        drain(band - 1)

    for q, (row, copy) in enumerate(copies(band)):
        for half in range(2):
            part = slice(half * elevations, (half + 1) * elevations)
            image_sc[q, :, part] = (step_sc[span[q], part] * factor_sc[...]).astype(image_sc.dtype)

        @pl.when(jnp.logical_and(row >= 0, row < own_rows))
        def _(copy=copy):
            copy.start()

    @pl.when(band == bands - 1)
    def _():
        drain(band)


def invert(targets, runs, back, ahead, own_rows, columns):
    lines = targets.shape[0]
    bands = runs.shape[0]
    elevations = back.shape[2] // 2
    whole = pl.BlockSpec(memory_space=pltpu.VMEM)
    pixels = BAND * columns
    tile_width = 256
    return pl.pallas_call(
        functools.partial(band_kernel, own_rows=own_rows, tile_width=tile_width),
        grid=(bands,),
        in_specs=[
            pl.BlockSpec((lines, pixels), lambda i: (0, i)),
            pl.BlockSpec((1, 1, columns), lambda i: (i, 0, 0)),
            whole,
            whole,
        ],
        out_specs=pl.BlockSpec(memory_space=pl.ANY),
        out_shape=jax.ShapeDtypeStruct((own_rows, columns, 2 * elevations), jnp.bfloat16),
        scratch_shapes=[
            pltpu.VMEM((pixels, lines), jnp.float32),
            pltpu.VMEM((pixels, lines), jnp.bfloat16),
            pltpu.VMEM((pixels, 2 * elevations), jnp.float32),
            pltpu.VMEM((columns, tile_width), jnp.float32),
            pltpu.VMEM((columns, elevations), jnp.float32),
            pltpu.VMEM((BAND, columns, 2 * elevations), jnp.bfloat16),
            pltpu.SemaphoreType.DMA((BAND,)),
        ],
        compiler_params=pltpu.CompilerParams(vmem_limit_bytes=40 * 1024 * 1024),
        name="invert",
    )(targets, runs, back, ahead)


def shifted(value, step):
    count = lax.axis_size("acq")
    pairs = [(i, i + step) for i in range(count) if 0 <= i + step < count]
    return lax.ppermute(value, "acq", pairs)


def steering_of(phase, acqs):
    acquisitions = phase.shape[1]
    scale = 1.0 / math.sqrt(acquisitions)
    real = (jnp.cos(phase) * scale).astype(jnp.bfloat16)
    imag = (jnp.sin(phase) * scale).astype(jnp.bfloat16)
    count = phase.shape[0]
    upper = jnp.concatenate([real, -imag], axis=2).reshape(count, -1, 1, acqs, 2 * phase.shape[2])
    lower = jnp.concatenate([imag, real], axis=2).reshape(count, -1, 1, acqs, 2 * phase.shape[2])
    return jnp.concatenate([upper, lower], axis=2).reshape(count, 2 * acquisitions, 2 * phase.shape[2])


def on_device(measurements, tile_order, steer_phase, group_ids):
    acqs = measurements.shape[0]
    rows, columns = group_ids.shape
    assert rows % BAND == 0
    sent = order_tiles(measurements, tile_order)
    targets = lax.all_to_all(sent, "acq", 0, 0, tiled=True)
    phase = jnp.concatenate([shifted(steer_phase, 1), steer_phase, shifted(steer_phase, -1)], axis=0)
    back = steering_of(phase, acqs)
    ahead = back.transpose(0, 2, 1)
    label_rows = [0] + [BAND * b - 1 for b in range(1, rows // BAND + 1)]
    starts = jnp.stack([group_ids[r] for r in label_rows]) % columns
    runs = ((starts + BAND - 1) // BAND)[:, None, :]
    edge = columns * (BAND - 1)
    extended = jnp.concatenate(
        [shifted(targets[:, -columns:], 1), targets, shifted(targets[:, :edge], -1)], axis=1
    )
    return invert(extended, runs, back * STEP_SIZE, ahead, rows, columns)


def solution(mesh):
    placed = (
        P(("groups", "acq"), None, None, None, None),
        P("groups"),
        P(("groups", "acq"), None, None),
        P(("groups", "acq"), None),
    )
    return jax.shard_map(
        on_device,
        mesh=mesh,
        in_specs=placed,
        out_specs=P(("groups", "acq"), None, None),
        check_vma=False,
    )
```

time: 187 us -> 73.6 us (0.39)
  the two profiles are of different devices: /device:TPU:14 before, /device:TPU:15 now
where the time goes in v1:
time: 73.6 us; the launch traced here: 73.1 us
  Pallas kernels  30.8 us (42%)
  starting transfers between devices  17.7 us (24%)
  waiting for transfers between devices  14.3 us (19%)
  other arithmetic  5.92 us (8%)
  local copies, waits for them, and re-layouts  4.23 us (6%)
    pallas_call x1, Pallas kernels, invert(): pl.pallas_call(functools.partial(band_kernel, own_rows=own_rows, tile_wid...  27.1 us
    ppermute x4, starting transfers between devices, shifted(): return lax.ppermute(value, 'acq', pairs)  11.2 us
    all_to_all x1, waiting for transfers between devices, on_device(): targets = lax.all_to_all(sent, 'acq', 0, 0, tiled=True)  9.54 us
    all_to_all x1, starting transfers between devices, on_device(): targets = lax.all_to_all(sent, 'acq', 0, 0, tiled=True)  6.45 us
    ppermute x4, waiting for transfers between devices, shifted(): return lax.ppermute(value, 'acq', pairs)  4.79 us
    pallas_call x1, Pallas kernels, order_tiles(): pl.pallas_call(order_kernel, grid=(rows // chunk,), in_specs=[pl.BlockSpe...  3.69 us
    unnamed x6, local copies, waits for them, and re-layouts  2.82 us
    neg x1, other arithmetic, steering_of(): -imag  2.69 us
  transfers between devices with their start and end apart: 5, of which 2 were waited for; matrix products, arithmetic and copies ran while one was open for 14% of the time, Pallas kernels for 5%

profile of v1, /device:TPU:15, one launch (start us, length us, event | category | flops | bytes accessed | tf_op | source)
XLA Modules:
  0.0 73.1 jit_solution(2656656455399456250)
XLA Ops:
  0.0 3.7 %collective-permute-start.2 = (f32[1,64,512]{2,1,0:T(8,128)}, f32[1,64,512]{2,1,0:T(8,128)S(1)}, u32[]{:S(2)}, u32[]{:S(2)}) collective-permute-start(f32[1,64,512]{2,1,0:T(8,128)} %param.6), channel_id=1, source_target_pairs={{0,1},{1,2},{2,3},{3,4},{4,5},{5,6},{6,7},{7,8},{8,9},{9,10},{10,1... | collective-permute-start | bytes 393224 | tf_op jit(solution)/shard_map/ppermute | solution.py:191
  3.7 1.9 %collective-permute-start.3 = (f32[1,64,512]{2,1,0:T(8,128)}, f32[1,64,512]{2,1,0:T(8,128)S(1)}, u32[]{:S(2)}, u32[]{:S(2)}) collective-permute-start(f32[1,64,512]{2,1,0:T(8,128)} %param.6), channel_id=1, source_target_pairs={{1,0},{2,1},{3,2},{4,3},{5,4},{6,5},{7,6},{8,7},{9,8},{10,9},{11,1... | collective-permute-start | bytes 393224 | tf_op jit(solution)/shard_map/ppermute | solution.py:191
  5.6 0.0 copy-start
  5.6 3.7 %order_tiles.1 = bf16[128,3072]{1,0:T(8,128)(2,1)} custom-call(s32[16]{0:T(128)} %order_ref.1, bf16[4,2,12,16,256]{4,3,2,1,0:T(8,128)(2,1)} %bitcast.28), custom_call_target="tpu_custom_call" | custom-call | tf_op jit(solution)/shard_map/order_tiles/pallas_call | solution.py:44
  9.3 6.5 %all-to-all-start = ((bf16[16,8,3072]{2,1,0:T(8,128)(2,1)}), bf16[16,8,3072]{2,1,0:T(8,128)(2,1)S(1)}, u32[]{:S(2)}, u32[]{:S(2)}) async-start(bf16[16,8,3072]{2,1,0:T(8,128)(2,1)} %bitcast.21), calls=%async_computation | async-start | bytes 1572864 | tf_op jit(solution)/shard_map/all_to_all | solution.py:210
  15.8 0.0 copy-done
  15.8 0.7 constant_dynamic-update-slice_fusion.4
  16.5 0.7 constant_dynamic-update-slice_fusion.3
  17.2 0.7 constant_dynamic-update-slice_fusion.2
  18.0 0.7 constant_dynamic-update-slice_fusion.1
  18.7 0.7 constant_dynamic-update-slice_fusion
  19.4 0.1 and_select_fusion.run_ref
  19.4 0.0 collective-permute-done.2
  19.5 0.0 collective-permute-done.3
  19.5 2.6 %multiply_convert_fusion.1 = bf16[3,16,1,4,512]{4,3,2,1,0:T(4,128)(2,1)S(1)} fusion(f32[1,16,1,4,512]{4,3,2,1,0:T(4,128)S(1)} %bitcast.26, f32[1,16,1,4,512]{4,3,2,1,0:T(4,128)S(1)} %bitcast.22, f32[1,16,1,4,512]{4,3,2,1,0:T(4,128)S(1)} %bitcast.24), kind=kLoop, calls=%fused_computation.5 | loop fusion | flops 393216 | bytes 589824 | tf_op jit(solution)/shard_map/convert_element_type | solution.py:197
  22.2 2.7 %fusion.2 = (bf16[3,16,1,4,512]{4,3,2,1,0:T(4,128)(2,1)S(1)}, bf16[3,16,1,4,512]{4,3,2,1,0:T(4,128)(2,1)S(1)}) fusion(f32[1,16,1,4,512]{4,3,2,1,0:T(4,128)S(1)} %bitcast.27, f32[1,16,1,4,512]{4,3,2,1,0:T(4,128)S(1)} %bitcast.23, f32[1,16,1,4,512]{4,3,2,1,0:T(4,128)S(1)} %bitcast.25), kind=kLoop, calls=%fused_computation.17 | loop fusion | flops 688128 | bytes 786432 | tf_op jit(solution)/shard_map/neg | solution.py:200
  24.8 0.4 maximum_maximum_fusion
  25.3 0.2 reshape.379
  25.5 9.5 %all-to-all-done = bf16[16,8,3072]{2,1,0:T(8,128)(2,1)S(1)} async-done(((bf16[16,8,3072]{2,1,0:T(8,128)(2,1)}), bf16[16,8,3072]{2,1,0:T(8,128)(2,1)S(1)}, u32[]{:S(2)}, u32[]{:S(2)}) %all-to-all-start) | async-done | bytes 786464 | tf_op jit(solution)/shard_map/all_to_all | solution.py:210
  35.1 3.7 %collective-permute-start = (bf16[128,256]{1,0:T(8,128)(2,1)S(1)}, bf16[128,256]{1,0:T(8,128)(2,1)S(1)}, u32[]{:S(2)}, u32[]{:S(2)}) collective-permute-start(bf16[128,256]{1,0:T(8,128)(2,1)S(1)} %slice.28), channel_id=1, source_target_pairs={{0,1},{1,2},{2,3},{3,4},{4,5},{5,6},{6,7},{7,8},{8,9},{9,10},{10,1... | collective-permute-start | bytes 196616 | tf_op jit(solution)/shard_map/ppermute | solution.py:191
  38.7 1.9 %collective-permute-start.1 = (bf16[128,512]{1,0:T(8,128)(2,1)S(1)}, bf16[128,512]{1,0:T(8,128)(2,1)S(1)}, u32[]{:S(2)}, u32[]{:S(2)}) collective-permute-start(bf16[128,512]{1,0:T(8,128)(2,1)S(1)} %slice.29), channel_id=1, source_target_pairs={{1,0},{2,1},{3,2},{4,3},{5,4},{6,5},{7,6},{8,7},{9,8},{10,9},{11,1... | collective-permute-start | bytes 393224 | tf_op jit(solution)/shard_map/ppermute | solution.py:191
  40.7 0.1 broadcast_multiply_fusion.back_ref
  40.7 0.4 copy.12
  41.1 0.0 collective-permute-done
  41.1 4.8 %collective-permute-done.1 = bf16[128,512]{1,0:T(8,128)(2,1)S(1)} collective-permute-done((bf16[128,512]{1,0:T(8,128)(2,1)S(1)}, bf16[128,512]{1,0:T(8,128)(2,1)S(1)}, u32[]{:S(2)}, u32[]{:S(2)}) %collective-permute-start.1) | collective-permute-done | bytes 131104 | tf_op jit(solution)/shard_map/ppermute | solution.py:191
  45.9 0.1 pad_maximum_fusion.target_ref
  46.0 27.1 %invert.1 = bf16[12,256,1024]{2,1,0:T(8,128)(2,1)} custom-call(bf16[128,3840]{1,0:T(8,128)(2,1)S(1)} %pad_maximum_fusion.target_ref, s32[5,1,256]{2,1,0:T(1,128)S(1)} %and_select_fusion.run_ref, bf16[3,128,1024]{2,1,0:T(8,128)(2,1)S(1)} %broadcast_multiply_fusion.back_ref, bf16[3,1024,128]{2,1,0:T(8,128)(2,1)S(1)} %bitcast.17), custom_call_target="tpu_custom_call" | custom-call | tf_op jit(solution)/shard_map/invert/pallas_call | solution.py:163
  (5 shorter events, 0.1 us)
Async XLA Ops:
  0.0 19.4 %collective-permute-start.2 = (f32[1,64,512]{2,1,0:T(8,128)}, f32[1,64,512]{2,1,0:T(8,128)S(1)}, u32[]{:S(2)}, u32[]{:S(2)}) collective-permute-start(f32[1,64,512]{2,1,0:T(8,128)} %param.6), channel_id=1, source_target_pairs={{0,1},{1,2},{2,3},{3,4},{4,5},{5,6},{6,7},{7,8},{8,9},{9,10},{10,1... | collective-permute-start | bytes 393224 | tf_op jit(solution)/shard_map/ppermute | solution.py:191
  3.7 15.8 %collective-permute-start.3 = (f32[1,64,512]{2,1,0:T(8,128)}, f32[1,64,512]{2,1,0:T(8,128)S(1)}, u32[]{:S(2)}, u32[]{:S(2)}) collective-permute-start(f32[1,64,512]{2,1,0:T(8,128)} %param.6), channel_id=1, source_target_pairs={{1,0},{2,1},{3,2},{4,3},{5,4},{6,5},{7,6},{8,7},{9,8},{10,9},{11,1... | collective-permute-start | bytes 393224 | tf_op jit(solution)/shard_map/ppermute | solution.py:191
  5.6 10.2 %copy-start = (f32[1,64,512]{2,1,0:T(8,128)S(1)}, f32[1,64,512]{2,1,0:T(8,128)}, u32[]{:S(2)}) copy-start(f32[1,64,512]{2,1,0:T(8,128)} %param.6) | copy-start | bytes 393220
  9.3 25.7 %all-to-all-start = ((bf16[16,8,3072]{2,1,0:T(8,128)(2,1)}), bf16[16,8,3072]{2,1,0:T(8,128)(2,1)S(1)}, u32[]{:S(2)}, u32[]{:S(2)}) async-start(bf16[16,8,3072]{2,1,0:T(8,128)(2,1)} %bitcast.21), calls=%async_computation | async-start | bytes 1572864 | tf_op jit(solution)/shard_map/all_to_all | solution.py:210
  35.1 6.1 %collective-permute-start = (bf16[128,256]{1,0:T(8,128)(2,1)S(1)}, bf16[128,256]{1,0:T(8,128)(2,1)S(1)}, u32[]{:S(2)}, u32[]{:S(2)}) collective-permute-start(bf16[128,256]{1,0:T(8,128)(2,1)S(1)} %slice.28), channel_id=1, source_target_pairs={{0,1},{1,2},{2,3},{3,4},{4,5},{5,6},{6,7},{7,8},{8,9},{9,10},{10,1... | collective-permute-start | bytes 196616 | tf_op jit(solution)/shard_map/ppermute | solution.py:191
  38.7 7.2 %collective-permute-start.1 = (bf16[128,512]{1,0:T(8,128)(2,1)S(1)}, bf16[128,512]{1,0:T(8,128)(2,1)S(1)}, u32[]{:S(2)}, u32[]{:S(2)}) collective-permute-start(bf16[128,512]{1,0:T(8,128)(2,1)S(1)} %slice.29), channel_id=1, source_target_pairs={{1,0},{2,1},{3,2},{4,3},{5,4},{6,5},{7,6},{8,7},{9,8},{10,9},{11,1... | collective-permute-start | bytes 393224 | tf_op jit(solution)/shard_map/ppermute | solution.py:191

commit v2 on v1

v2 whole, which is shorter than its diff:
```python
import functools
import math

import jax
import jax.numpy as jnp
from jax import lax
from jax.experimental import pallas as pl
from jax.experimental.pallas import tpu as pltpu
from jax.sharding import PartitionSpec as P


ITERS = 3
BAND = 3
STEP_SIZE = 0.0625
SHRINK_LEVEL = 3.0


def dot(a, b, dims=((1,), (0,))):
    return lax.dot_general(a, b, (dims, ((), ())), preferred_element_type=jnp.float32)


def order_kernel(order_ref, *refs, spans):
    stack_ref, sent_refs = refs[0], refs[1:]
    acqs, parts, _, tiles, columns = stack_ref.shape
    lines = acqs * parts * tiles
    share = acqs * parts
    target = lax.broadcasted_iota(jnp.int32, (lines, 1), 0)
    source = lax.broadcasted_iota(jnp.int32, (1, lines), 1)
    block = lax.rem(source, tiles)
    part = lax.rem(lax.div(source, tiles), parts)
    acq = lax.div(source, tiles * parts)
    tile = jnp.zeros((1, lines), jnp.int32)
    for k in range(tiles):
        tile = jnp.where(block == k, order_ref[k], tile)
    place = tile * share + part * acqs + acq
    pick = jnp.where(target == place, 1.0, 0.0).astype(jnp.bfloat16)
    for sent_ref, span in zip(sent_refs, spans):
        for q, row in enumerate(span):
            lump = stack_ref[:, :, row].reshape(lines, columns)
            sent_ref[:, q * columns : (q + 1) * columns] = dot(pick, lump).astype(sent_ref.dtype)


def order_tiles(measurements, tile_order, spans):
    acqs, parts, tiles, _, columns = measurements.shape
    stack = measurements.transpose(0, 1, 3, 2, 4)
    lines = acqs * parts * tiles
    whole = pl.BlockSpec(memory_space=pltpu.VMEM)
    return pl.pallas_call(
        functools.partial(order_kernel, spans=spans),
        in_specs=[pl.BlockSpec(memory_space=pltpu.SMEM), whole],
        out_specs=[whole] * len(spans),
        out_shape=[
            jax.ShapeDtypeStruct((lines, len(span) * columns), measurements.dtype) for span in spans
        ],
        name="order_tiles",
    )(tile_order, stack)


def shrink_factor(energy, pick):
    sums = dot(pick, energy.astype(jnp.bfloat16))
    factor = jnp.maximum(1.0 - SHRINK_LEVEL * lax.rsqrt(jnp.maximum(sums, SHRINK_LEVEL**2)), 0.0)
    high = factor.astype(jnp.bfloat16)
    low = (factor - high.astype(jnp.float32)).astype(jnp.bfloat16)
    both = jnp.concatenate([high, low], axis=0)
    return dot(jnp.concatenate([pick, pick], axis=0), both, ((0,), (0,)))


def band_kernel(
    target_ref, run_ref, back_ref, ahead_ref, *refs, stride, base, tile_width,
):
    out_ref, target_sc, resid_sc, state_sc, energy_sc, factor_sc, guess_sc, image_sc, sem = refs[-9:]
    own_rows = out_ref.shape[0]
    last_band = own_rows // BAND
    step = pl.program_id(0)
    steps = pl.num_programs(0)
    band = step * stride + base
    columns = run_ref.shape[2]
    elevations = factor_sc.shape[1]
    groups = pick_height(columns)
    weight_of = (1,) * BAND if stride != last_band else (step,) + (step + 1,) * (BAND - 1)
    span = [slice(q * columns, (q + 1) * columns) for q in range(BAND)]
    tiles = [
        (slice(at, at + tile_width), slice(elevations + at, elevations + at + tile_width))
        for at in range(0, elevations, tile_width)
    ]

    def copies(of):
        return [
            (of * BAND + q - 1, pltpu.make_async_copy(
                image_sc.at[q], out_ref.at[jnp.clip(of * BAND + q - 1, 0, own_rows - 1)], sem.at[q]))
            for q in range(BAND)
        ]

    def drain(of):
        for row, copy in copies(of):
            @pl.when(jnp.logical_and(row >= 0, row < own_rows))
            def _(copy=copy):
                copy.wait()

    group = lax.broadcasted_iota(jnp.int32, (groups, columns), 0)
    pick = jnp.where(group == run_ref[0], 1.0, 0.0).astype(jnp.bfloat16)
    target_sc[...] = target_ref[...].T

    @pl.when(step > 0)
    def _():
        drain(band - stride)

    for i in range(ITERS):
        for t, (real, imag) in enumerate(tiles):
            for q in range(BAND):
                resid = target_sc[span[q]] if i == 0 else resid_sc[span[q]]
                step_real = dot(resid, back_ref[weight_of[q], :, real])
                step_imag = dot(resid, back_ref[weight_of[q], :, imag])
                if i > 0:
                    step_real += state_sc[span[q], real]
                    step_imag += state_sc[span[q], imag]
                state_sc[span[q], real] = step_real
                state_sc[span[q], imag] = step_imag
                energy = step_real * step_real + step_imag * step_imag
                if q > 0:
                    energy += energy_sc[t]
                if q < BAND - 1:
                    energy_sc[t] = energy
            factor_sc[:, real] = shrink_factor(energy, pick)
            for q in range(BAND):
                factor = factor_sc[:, real]
                new_real = state_sc[span[q], real] * factor
                new_imag = state_sc[span[q], imag] * factor
                if i == ITERS - 1:
                    image_sc[q, :, real] = new_real.astype(image_sc.dtype)
                    image_sc[q, :, imag] = new_imag.astype(image_sc.dtype)
                    continue
                state_sc[span[q], real] = new_real
                state_sc[span[q], imag] = new_imag
                rounded = jnp.concatenate([new_real, new_imag], axis=1).astype(jnp.bfloat16)
                weights = jnp.concatenate(
                    [ahead_ref[weight_of[q], real], ahead_ref[weight_of[q], imag]], axis=0
                )
                guess = dot(rounded, weights)
                if t > 0:
                    guess += guess_sc[span[q]]
                if t < len(tiles) - 1:
                    guess_sc[span[q]] = guess
                else:
                    resid_sc[span[q]] = (target_sc[span[q]].astype(jnp.float32) - guess).astype(
                        jnp.bfloat16
                    )

    for row, copy in copies(band):
        @pl.when(jnp.logical_and(row >= 0, row < own_rows))
        def _(copy=copy):
            copy.start()

    @pl.when(step == steps - 1)
    def _():
        drain(band)


def pick_height(columns):
    return -(-(columns // BAND + 2) // 16) * 16


def invert(targets, runs, back, ahead, out, out_shape, base, stride):
    lines = targets.shape[0]
    steps = runs.shape[0]
    columns = runs.shape[2]
    elevations = back.shape[2] // 2
    whole = pl.BlockSpec(memory_space=pltpu.VMEM)
    far = pl.BlockSpec(memory_space=pl.ANY)
    pixels = BAND * columns
    tile_width = 256
    held = () if out is None else (out,)
    return pl.pallas_call(
        functools.partial(band_kernel, base=base, stride=stride, tile_width=tile_width),
        grid=(steps,),
        in_specs=[
            pl.BlockSpec((lines, pixels), lambda i: (0, i)),
            pl.BlockSpec((1, 1, columns), lambda i: (i, 0, 0)),
            whole,
            whole,
        ]
        + [far] * len(held),
        out_specs=far,
        out_shape=jax.ShapeDtypeStruct(out_shape, jnp.bfloat16),
        input_output_aliases={4: 0} if held else {},
        scratch_shapes=[
            pltpu.VMEM((pixels, lines), jnp.bfloat16),
            pltpu.VMEM((pixels, lines), jnp.bfloat16),
            pltpu.VMEM((pixels, 2 * elevations), jnp.float32),
            pltpu.VMEM((elevations // tile_width, columns, tile_width), jnp.float32),
            pltpu.VMEM((columns, elevations), jnp.float32),
            pltpu.VMEM((pixels, lines), jnp.float32),
            pltpu.VMEM((BAND, columns, 2 * elevations), jnp.bfloat16),
            pltpu.SemaphoreType.DMA((BAND,)),
        ],
        compiler_params=pltpu.CompilerParams(vmem_limit_bytes=40 * 1024 * 1024),
        name="invert",
    )(targets, runs, back, ahead, *held)


def shifted(value, step):
    count = lax.axis_size("acq")
    pairs = [(i, i + step) for i in range(count) if 0 <= i + step < count]
    return lax.ppermute(value, "acq", pairs)


def steering_of(phase, acqs):
    acquisitions = phase.shape[1]
    scale = 1.0 / math.sqrt(acquisitions)
    real = (jnp.cos(phase) * scale).astype(jnp.bfloat16)
    imag = (jnp.sin(phase) * scale).astype(jnp.bfloat16)
    count = phase.shape[0]
    upper = jnp.concatenate([real, -imag], axis=2).reshape(count, -1, 1, acqs, 2 * phase.shape[2])
    lower = jnp.concatenate([imag, real], axis=2).reshape(count, -1, 1, acqs, 2 * phase.shape[2])
    return jnp.concatenate([upper, lower], axis=2).reshape(count, 2 * acquisitions, 2 * phase.shape[2])


def program(measurements, tile_order, steer_phase, group_ids):
    acqs = measurements.shape[0]
    rows, columns = group_ids.shape
    elevations = steer_phase.shape[2]
    assert rows % BAND == 0
    bands = rows // BAND
    edge = [rows - 1] + list(range(BAND - 1))
    inner = [list(range(BAND * b - 1, BAND * b + 2)) for b in range(1, bands)]
    early = 1
    spans = [edge + sum(inner[:early], []), sum(inner[early:], [])]
    sent = order_tiles(measurements, tile_order, spans)
    head = lax.all_to_all(sent[0], "acq", 0, 0, tiled=True)
    tail = lax.all_to_all(sent[1], "acq", 0, 0, tiled=True)
    phase = jnp.concatenate(
        [shifted(steer_phase, 1), steer_phase, shifted(steer_phase, -1)], axis=0
    )
    back = steering_of(phase, acqs)
    ahead = back.transpose(0, 2, 1)
    back = back * STEP_SIZE
    runs = ((group_ids % columns + BAND - 1) // BAND)[:, None, :]
    runs_of = [runs[max(BAND * b - 1, 0)] for b in range(bands + 1)]
    width = BAND * columns
    above, below = head[:, :columns], head[:, columns:width]
    targets = jnp.concatenate([shifted(above, 1), below, above, shifted(below, -1)], axis=1)
    shape = (rows, columns, 2 * elevations)
    out = invert(targets, jnp.stack([runs_of[0], runs_of[-1]]), back, ahead, None, shape, 0, bands)
    mine = jnp.stack(runs_of[1 : 1 + early])
    out = invert(head[:, width:], mine, back, ahead, out, shape, 1, 1)
    mine = jnp.stack(runs_of[1 + early : bands])
    out = invert(tail, mine, back, ahead, out, shape, 1 + early, 1)
    return out


def solution(mesh):
    placed = (
        P(("groups", "acq"), None, None, None, None),
        P("groups"),
        P(("groups", "acq"), None, None),
        P(("groups", "acq"), None),
    )
    return jax.shard_map(
        program,
        mesh=mesh,
        in_specs=placed,
        out_specs=P(("groups", "acq"), None, None),
        check_vma=False,
    )
```

time: 73.6 us -> 75.2 us (1.022)
  the two profiles are of different devices: /device:TPU:15 before, /device:TPU:7 now
where the time goes in v2:
time: 75.2 us; the launch traced here: 74.8 us
  Pallas kernels  32.7 us (43%)
  starting transfers between devices  22.3 us (30%)
  waiting for transfers between devices  12.8 us (17%)
  other arithmetic  5.86 us (8%)
    pallas_call x3, Pallas kernels, invert(): pl.pallas_call(functools.partial(band_kernel, base=base, stride=stride, t...  30.5 us
    ppermute x4, starting transfers between devices, shifted(): return lax.ppermute(value, 'acq', pairs)  11.2 us
    all_to_all x1, waiting for transfers between devices, program(): head = lax.all_to_all(sent[0], 'acq', 0, 0, tiled=True)  8.2 us
    all_to_all x1, starting transfers between devices, program(): head = lax.all_to_all(sent[0], 'acq', 0, 0, tiled=True)  6.57 us
    ppermute x4, waiting for transfers between devices, shifted(): return lax.ppermute(value, 'acq', pairs)  4.59 us
    all_to_all x1, starting transfers between devices, program(): tail = lax.all_to_all(sent[1], 'acq', 0, 0, tiled=True)  4.48 us
    neg x1, other arithmetic, steering_of(): -imag  2.69 us
    convert_element_type x1, other arithmetic, steering_of(): real = (jnp.cos(phase) * scale).astype(jnp.bfloat16)  2.59 us
  transfers between devices with their start and end apart: 6, of which 2 were waited for; matrix products, arithmetic and copies ran while one was open for 9% of the time, Pallas kernels for 27%

profile of v2, /device:TPU:7, one launch (start us, length us, event | category | flops | bytes accessed | tf_op | source)
XLA Modules:
  0.0 74.8 jit_solution(15072035520653053358)
XLA Ops:
  0.0 0.0 copy-start
  0.0 0.0 copy-start.1
  0.0 3.8 %collective-permute-start = (f32[1,64,512]{2,1,0:T(8,128)}, f32[1,64,512]{2,1,0:T(8,128)S(1)}, u32[]{:S(2)}, u32[]{:S(2)}) collective-permute-start(f32[1,64,512]{2,1,0:T(8,128)} %param.6), channel_id=1, source_target_pairs={{0,1},{1,2},{2,3},{3,4},{4,5},{5,6},{6,7},{7,8},{8,9},{9,10},{10,1... | collective-permute-start | bytes 393224 | tf_op jit(solution)/shard_map/ppermute | solution.py:204
  3.8 1.9 %collective-permute-start.1 = (f32[1,64,512]{2,1,0:T(8,128)}, f32[1,64,512]{2,1,0:T(8,128)S(1)}, u32[]{:S(2)}, u32[]{:S(2)}) collective-permute-start(f32[1,64,512]{2,1,0:T(8,128)} %param.6), channel_id=1, source_target_pairs={{1,0},{2,1},{3,2},{4,3},{5,4},{6,5},{7,6},{8,7},{9,8},{10,9},{11,1... | collective-permute-start | bytes 393224 | tf_op jit(solution)/shard_map/ppermute | solution.py:204
  5.8 2.3 %order_tiles.1 = (bf16[128,1536]{1,0:T(8,128)(2,1)}, bf16[128,1536]{1,0:T(8,128)(2,1)}) custom-call(s32[16]{0:T(128)} %order_ref.1, bf16[4,2,12,16,256]{4,3,2,1,0:T(8,128)(2,1)} %bitcast.32), custom_call_target="tpu_custom_call" | custom-call | tf_op jit(solution)/shard_map/order_tiles/pallas_call | solution.py:48
  8.0 6.6 %all-to-all-start.1 = ((bf16[16,8,1536]{2,1,0:T(8,128)(2,1)}), bf16[16,8,1536]{2,1,0:T(8,128)(2,1)S(1)}, u32[]{:S(2)}, u32[]{:S(2)}) async-start(bf16[16,8,1536]{2,1,0:T(8,128)(2,1)} %bitcast.33), calls=%async_computation.1 | async-start | bytes 786432 | tf_op jit(solution)/shard_map/all_to_all | solution.py:229
  14.6 0.0 copy-done.1
  14.7 0.0 copy-done
  14.7 0.0 collective-permute-done
  14.8 0.0 collective-permute-done.1
  14.8 2.7 %fusion.3 = (bf16[3,16,1,4,512]{4,3,2,1,0:T(4,128)(2,1)S(1)}, bf16[3,16,1,4,512]{4,3,2,1,0:T(4,128)(2,1)S(1)}) fusion(f32[1,16,1,4,512]{4,3,2,1,0:T(4,128)S(1)} %bitcast.30, f32[1,16,1,4,512]{4,3,2,1,0:T(4,128)S(1)} %bitcast.26, f32[1,16,1,4,512]{4,3,2,1,0:T(4,128)S(1)} %bitcast.28), kind=kLoop, calls=%fused_computation.22 | loop fusion | flops 688128 | bytes 786432 | tf_op jit(solution)/shard_map/neg | solution.py:213
  17.5 8.2 %all-to-all-done.1 = bf16[16,8,1536]{2,1,0:T(8,128)(2,1)S(1)} async-done(((bf16[16,8,1536]{2,1,0:T(8,128)(2,1)}), bf16[16,8,1536]{2,1,0:T(8,128)(2,1)S(1)}, u32[]{:S(2)}, u32[]{:S(2)}) %all-to-all-start.1) | async-done | bytes 393248 | tf_op jit(solution)/shard_map/all_to_all | solution.py:229
  25.7 4.5 %all-to-all-start = ((bf16[16,8,1536]{2,1,0:T(8,128)(2,1)}), bf16[16,8,1536]{2,1,0:T(8,128)(2,1)S(1)}, u32[]{:S(2)}, u32[]{:S(2)}) async-start(bf16[16,8,1536]{2,1,0:T(8,128)(2,1)} %bitcast.1), calls=%async_computation | async-start | bytes 786432 | tf_op jit(solution)/shard_map/all_to_all | solution.py:230
  30.2 2.6 %multiply_convert_fusion.1 = bf16[3,16,1,4,512]{4,3,2,1,0:T(4,128)(2,1)S(1)} fusion(f32[1,16,1,4,512]{4,3,2,1,0:T(4,128)S(1)} %bitcast.31, f32[1,16,1,4,512]{4,3,2,1,0:T(4,128)S(1)} %bitcast.27, f32[1,16,1,4,512]{4,3,2,1,0:T(4,128)S(1)} %bitcast.29), kind=kLoop, calls=%fused_computation.5 | loop fusion | flops 393216 | bytes 589824 | tf_op jit(solution)/shard_map/convert_element_type | solution.py:210
  32.8 0.5 maximum_maximum_fusion
  33.3 0.2 reshape.141
  33.5 3.4 %collective-permute-start.2 = (bf16[128,256]{1,0:T(8,128)(2,1)S(1)}, bf16[128,256]{1,0:T(8,128)(2,1)S(1)}, u32[]{:S(2)}, u32[]{:S(2)}) collective-permute-start(bf16[128,256]{1,0:T(8,128)(2,1)S(1)} %slice.56), channel_id=1, source_target_pairs={{0,1},{1,2},{2,3},{3,4},{4,5},{5,6},{6,7},{7,8},{8,9},{9,10},{10,1... | collective-permute-start | bytes 196616 | tf_op jit(solution)/shard_map/ppermute | solution.py:204
  36.9 2.1 %collective-permute-start.3 = (bf16[128,512]{1,0:T(8,128)(2,1)S(1)}, bf16[128,512]{1,0:T(8,128)(2,1)S(1)}, u32[]{:S(2)}, u32[]{:S(2)}) collective-permute-start(bf16[128,512]{1,0:T(8,128)(2,1)S(1)} %slice.57), channel_id=1, source_target_pairs={{1,0},{2,1},{3,2},{4,3},{5,4},{6,5},{7,6},{8,7},{9,8},{10,9},{11,1... | collective-permute-start | bytes 393224 | tf_op jit(solution)/shard_map/ppermute | solution.py:204
  39.0 0.1 broadcast_multiply_fusion.back_ref
  39.1 0.4 copy.16
  39.5 0.0 collective-permute-done.2
  39.5 4.6 %collective-permute-done.3 = bf16[128,512]{1,0:T(8,128)(2,1)S(1)} collective-permute-done((bf16[128,512]{1,0:T(8,128)(2,1)S(1)}, bf16[128,512]{1,0:T(8,128)(2,1)S(1)}, u32[]{:S(2)}, u32[]{:S(2)}) %collective-permute-start.3) | collective-permute-done | bytes 131104 | tf_op jit(solution)/shard_map/ppermute | solution.py:204
  44.1 11.9 %invert.3.refs_0_ = bf16[12,256,1024]{2,1,0:T(8,128)(2,1)} custom-call(bf16[128,1536]{1,0:T(8,128)(2,1)S(1)} %pad_maximum_fusion.1.target_ref, s32[2,1,256]{2,1,0:T(1,128)S(1)} %pad_add_fusion.1.run_ref, bf16[3,128,1024]{2,1,0:T(8,128)(2,1)S(1)} %broadcast_multiply_fusion.back_ref, bf16[3,1024,128]{2,1,0:T(8,128)(2,1)S(1)} %bitcast.19), custom_call_target="tpu_custom_call" | custom-call | tf_op jit(solution)/shard_map/invert/pallas_call | solution.py:173
  56.0 6.2 %invert.4.refs_0_ = bf16[12,256,1024]{2,1,0:T(8,128)(2,1)} custom-call(bf16[128,768]{1,0:T(8,128)(2,1)S(1)} %slice.54.target_ref, s32[1,1,256]{2,1,0:T(1,128)S(1)} %get-tuple-element.13.run_ref, bf16[3,128,1024]{2,1,0:T(8,128)(2,1)S(1)} %broadcast_multiply_fusion.back_ref, bf16[3,1024,128]{2,1,0:T(8,128)(2,1)S(1)} %bitcast.20, ...), custom_call_target="tpu_custom_call", output_to_operand_aliasing={{}: (4, {})} | custom-call | tf_op jit(solution)/shard_map/invert/pallas_call | solution.py:173
  62.2 0.0 all-to-all-done
  62.2 12.4 %invert.5 = bf16[12,256,1024]{2,1,0:T(8,128)(2,1)} custom-call(bf16[128,1536]{1,0:T(8,128)(2,1)S(1)} %bitcast.22, s32[2,1,256]{2,1,0:T(1,128)S(1)} %pad_add_fusion.run_ref, bf16[3,128,1024]{2,1,0:T(8,128)(2,1)S(1)} %broadcast_multiply_fusion.back_ref, bf16[3,1024,128]{2,1,0:T(8,128)(2,1)S(1)} %bitcast.21, ...), custom_call_target="tpu_custom_call", output_to_operand_aliasing={{}: (4, {})} | custom-call | tf_op jit(solution)/shard_map/invert/pallas_call | solution.py:173
  (11 shorter events, 0.2 us)
Async XLA Ops:
  0.0 14.7 %copy-start = (f32[1,64,512]{2,1,0:T(8,128)S(1)}, f32[1,64,512]{2,1,0:T(8,128)}, u32[]{:S(2)}) copy-start(f32[1,64,512]{2,1,0:T(8,128)} %param.6) | copy-start | bytes 393220
  0.0 14.6 %copy-start.1 = (s32[12,256]{1,0:T(8,128)S(1)}, s32[12,256]{1,0:T(8,128)}, u32[]{:S(2)}) copy-start(s32[12,256]{1,0:T(8,128)} %param.7) | copy-start | bytes 36868
  0.0 14.7 %collective-permute-start = (f32[1,64,512]{2,1,0:T(8,128)}, f32[1,64,512]{2,1,0:T(8,128)S(1)}, u32[]{:S(2)}, u32[]{:S(2)}) collective-permute-start(f32[1,64,512]{2,1,0:T(8,128)} %param.6), channel_id=1, source_target_pairs={{0,1},{1,2},{2,3},{3,4},{4,5},{5,6},{6,7},{7,8},{8,9},{9,10},{10,1... | collective-permute-start | bytes 393224 | tf_op jit(solution)/shard_map/ppermute | solution.py:204
  3.8 11.0 %collective-permute-start.1 = (f32[1,64,512]{2,1,0:T(8,128)}, f32[1,64,512]{2,1,0:T(8,128)S(1)}, u32[]{:S(2)}, u32[]{:S(2)}) collective-permute-start(f32[1,64,512]{2,1,0:T(8,128)} %param.6), channel_id=1, source_target_pairs={{1,0},{2,1},{3,2},{4,3},{5,4},{6,5},{7,6},{8,7},{9,8},{10,9},{11,1... | collective-permute-start | bytes 393224 | tf_op jit(solution)/shard_map/ppermute | solution.py:204
  8.0 17.7 %all-to-all-start.1 = ((bf16[16,8,1536]{2,1,0:T(8,128)(2,1)}), bf16[16,8,1536]{2,1,0:T(8,128)(2,1)S(1)}, u32[]{:S(2)}, u32[]{:S(2)}) async-start(bf16[16,8,1536]{2,1,0:T(8,128)(2,1)} %bitcast.33), calls=%async_computation.1 | async-start | bytes 786432 | tf_op jit(solution)/shard_map/all_to_all | solution.py:229
  25.7 36.5 %all-to-all-start = ((bf16[16,8,1536]{2,1,0:T(8,128)(2,1)}), bf16[16,8,1536]{2,1,0:T(8,128)(2,1)S(1)}, u32[]{:S(2)}, u32[]{:S(2)}) async-start(bf16[16,8,1536]{2,1,0:T(8,128)(2,1)} %bitcast.1), calls=%async_computation | async-start | bytes 786432 | tf_op jit(solution)/shard_map/all_to_all | solution.py:230
  33.5 6.0 %collective-permute-start.2 = (bf16[128,256]{1,0:T(8,128)(2,1)S(1)}, bf16[128,256]{1,0:T(8,128)(2,1)S(1)}, u32[]{:S(2)}, u32[]{:S(2)}) collective-permute-start(bf16[128,256]{1,0:T(8,128)(2,1)S(1)} %slice.56), channel_id=1, source_target_pairs={{0,1},{1,2},{2,3},{3,4},{4,5},{5,6},{6,7},{7,8},{8,9},{9,10},{10,1... | collective-permute-start | bytes 196616 | tf_op jit(solution)/shard_map/ppermute | solution.py:204
  36.9 7.2 %collective-permute-start.3 = (bf16[128,512]{1,0:T(8,128)(2,1)S(1)}, bf16[128,512]{1,0:T(8,128)(2,1)S(1)}, u32[]{:S(2)}, u32[]{:S(2)}) collective-permute-start(bf16[128,512]{1,0:T(8,128)(2,1)S(1)} %slice.57), channel_id=1, source_target_pairs={{1,0},{2,1},{3,2},{4,3},{5,4},{6,5},{7,6},{8,7},{9,8},{10,9},{11,1... | collective-permute-start | bytes 393224 | tf_op jit(solution)/shard_map/ppermute | solution.py:204

commit v3 on v2

--- a/solution.py
+++ b/solution.py
@@ -68,7 +68,7 @@
 def band_kernel(
     target_ref, run_ref, back_ref, ahead_ref, *refs, stride, base, tile_width,
 ):
-    out_ref, target_sc, resid_sc, state_sc, energy_sc, factor_sc, guess_sc, image_sc, sem = refs[-9:]
+    out_ref, target_sc, resid_sc, step_sc, energy_sc, factor_sc, image_sc, sem = refs[-8:]
     own_rows = out_ref.shape[0]
     last_band = own_rows // BAND
     step = pl.program_id(0)
@@ -76,13 +76,9 @@
     band = step * stride + base
     columns = run_ref.shape[2]
     elevations = factor_sc.shape[1]
-    groups = pick_height(columns)
+    groups = -(-(columns // BAND + 2) // 16) * 16
     weight_of = (1,) * BAND if stride != last_band else (step,) + (step + 1,) * (BAND - 1)
     span = [slice(q * columns, (q + 1) * columns) for q in range(BAND)]
-    tiles = [
-        (slice(at, at + tile_width), slice(elevations + at, elevations + at + tile_width))
-        for at in range(0, elevations, tile_width)
-    ]
 
     def copies(of):
         return [
@@ -99,54 +95,57 @@
 
     group = lax.broadcasted_iota(jnp.int32, (groups, columns), 0)
     pick = jnp.where(group == run_ref[0], 1.0, 0.0).astype(jnp.bfloat16)
-    target_sc[...] = target_ref[...].T
+    target_sc[...] = target_ref[...].astype(jnp.float32).T
+
+    def descend(is_first):
+        for at in range(0, elevations, tile_width):
+            real = slice(at, at + tile_width)
+            imag = slice(elevations + at, elevations + at + tile_width)
+            for q in range(BAND):
+                if is_first:
+                    resid = target_sc[span[q]].astype(jnp.bfloat16)
+                else:
+                    resid = resid_sc[span[q]]
+                step_real = dot(resid, back_ref[weight_of[q], :, real])
+                step_imag = dot(resid, back_ref[weight_of[q], :, imag])
+                if not is_first:
+                    factor = factor_sc[:, real]
+                    step_real += step_sc[span[q], real] * factor
+                    step_imag += step_sc[span[q], imag] * factor
+                step_sc[span[q], real] = step_real
+                step_sc[span[q], imag] = step_imag
+                energy = step_real * step_real + step_imag * step_imag
+                if q > 0:
+                    energy += energy_sc[...]
+                if q < BAND - 1:
+                    energy_sc[...] = energy
+            factor_sc[:, real] = shrink_factor(energy, pick)
+
+    def predict():
+        for q in range(BAND):
+            guess = jnp.zeros((columns, target_sc.shape[1]), jnp.float32)
+            for half in range(2):
+                part = slice(half * elevations, (half + 1) * elevations)
+                rounded = (step_sc[span[q], part] * factor_sc[...]).astype(jnp.bfloat16)
+                guess += dot(rounded, ahead_ref[weight_of[q], part])
+            resid_sc[span[q]] = (target_sc[span[q]] - guess).astype(jnp.bfloat16)
+
+    descend(True)
+
+    @pl.loop(1, ITERS)
+    def _(i):
+        predict()
+        descend(False)
 
     @pl.when(step > 0)
     def _():
         drain(band - stride)
 
-    for i in range(ITERS):
-        for t, (real, imag) in enumerate(tiles):
-            for q in range(BAND):
-                resid = target_sc[span[q]] if i == 0 else resid_sc[span[q]]
-                step_real = dot(resid, back_ref[weight_of[q], :, real])
-                step_imag = dot(resid, back_ref[weight_of[q], :, imag])
-                if i > 0:
-                    step_real += state_sc[span[q], real]
-                    step_imag += state_sc[span[q], imag]
-                state_sc[span[q], real] = step_real
-                state_sc[span[q], imag] = step_imag
-                energy = step_real * step_real + step_imag * step_imag
-                if q > 0:
-                    energy += energy_sc[t]
-                if q < BAND - 1:
-                    energy_sc[t] = energy
-            factor_sc[:, real] = shrink_factor(energy, pick)
-            for q in range(BAND):
-                factor = factor_sc[:, real]
-                new_real = state_sc[span[q], real] * factor
-                new_imag = state_sc[span[q], imag] * factor
-                if i == ITERS - 1:
-                    image_sc[q, :, real] = new_real.astype(image_sc.dtype)
-                    image_sc[q, :, imag] = new_imag.astype(image_sc.dtype)
-                    continue
-                state_sc[span[q], real] = new_real
-                state_sc[span[q], imag] = new_imag
-                rounded = jnp.concatenate([new_real, new_imag], axis=1).astype(jnp.bfloat16)
-                weights = jnp.concatenate(
-                    [ahead_ref[weight_of[q], real], ahead_ref[weight_of[q], imag]], axis=0
-                )
-                guess = dot(rounded, weights)
-                if t > 0:
-                    guess += guess_sc[span[q]]
-                if t < len(tiles) - 1:
-                    guess_sc[span[q]] = guess
-                else:
-                    resid_sc[span[q]] = (target_sc[span[q]].astype(jnp.float32) - guess).astype(
-                        jnp.bfloat16
-                    )
-
-    for row, copy in copies(band):
+    for q, (row, copy) in enumerate(copies(band)):
+        for half in range(2):
+            part = slice(half * elevations, (half + 1) * elevations)
+            image_sc[q, :, part] = (step_sc[span[q], part] * factor_sc[...]).astype(image_sc.dtype)
+
         @pl.when(jnp.logical_and(row >= 0, row < own_rows))
         def _(copy=copy):
             copy.start()
@@ -154,10 +153,6 @@
     @pl.when(step == steps - 1)
     def _():
         drain(band)
-
-
-def pick_height(columns):
-    return -(-(columns // BAND + 2) // 16) * 16
 
 
 def invert(targets, runs, back, ahead, out, out_shape, base, stride):
@@ -184,12 +179,11 @@
         out_shape=jax.ShapeDtypeStruct(out_shape, jnp.bfloat16),
         input_output_aliases={4: 0} if held else {},
         scratch_shapes=[
-            pltpu.VMEM((pixels, lines), jnp.bfloat16),
+            pltpu.VMEM((pixels, lines), jnp.float32),
             pltpu.VMEM((pixels, lines), jnp.bfloat16),
             pltpu.VMEM((pixels, 2 * elevations), jnp.float32),
-            pltpu.VMEM((elevations // tile_width, columns, tile_width), jnp.float32),
+            pltpu.VMEM((columns, tile_width), jnp.float32),
             pltpu.VMEM((columns, elevations), jnp.float32),
-            pltpu.VMEM((pixels, lines), jnp.float32),
             pltpu.VMEM((BAND, columns, 2 * elevations), jnp.bfloat16),
             pltpu.SemaphoreType.DMA((BAND,)),
         ],
@@ -204,15 +198,19 @@
     return lax.ppermute(value, "acq", pairs)
 
 
-def steering_of(phase, acqs):
-    acquisitions = phase.shape[1]
-    scale = 1.0 / math.sqrt(acquisitions)
+def steering_of(phase):
+    scale = 1.0 / math.sqrt(phase.shape[1])
     real = (jnp.cos(phase) * scale).astype(jnp.bfloat16)
     imag = (jnp.sin(phase) * scale).astype(jnp.bfloat16)
-    count = phase.shape[0]
-    upper = jnp.concatenate([real, -imag], axis=2).reshape(count, -1, 1, acqs, 2 * phase.shape[2])
-    lower = jnp.concatenate([imag, real], axis=2).reshape(count, -1, 1, acqs, 2 * phase.shape[2])
-    return jnp.concatenate([upper, lower], axis=2).reshape(count, 2 * acquisitions, 2 * phase.shape[2])
+    return jnp.concatenate([real, imag], axis=1)
+
+
+def planes_of(steering, acqs):
+    count, lines, elevations = steering.shape
+    real, imag = steering[:, : lines // 2], steering[:, lines // 2 :]
+    upper = jnp.concatenate([real, -imag], axis=2).reshape(count, -1, 1, acqs, 2 * elevations)
+    lower = jnp.concatenate([imag, real], axis=2).reshape(count, -1, 1, acqs, 2 * elevations)
+    return jnp.concatenate([upper, lower], axis=2).reshape(count, lines, 2 * elevations)
 
 
 def program(measurements, tile_order, steer_phase, group_ids):
@@ -228,10 +226,9 @@
     sent = order_tiles(measurements, tile_order, spans)
     head = lax.all_to_all(sent[0], "acq", 0, 0, tiled=True)
     tail = lax.all_to_all(sent[1], "acq", 0, 0, tiled=True)
-    phase = jnp.concatenate(
-        [shifted(steer_phase, 1), steer_phase, shifted(steer_phase, -1)], axis=0
-    )
-    back = steering_of(phase, acqs)
+    mine = steering_of(steer_phase)
+    steering = jnp.concatenate([shifted(mine, 1), mine, shifted(mine, -1)], axis=0)
+    back = planes_of(steering, acqs)
     ahead = back.transpose(0, 2, 1)
     back = back * STEP_SIZE
     runs = ((group_ids % columns + BAND - 1) // BAND)[:, None, :]

time: 75.2 us -> 72.4 us (0.963)
  the two profiles are of different devices: /device:TPU:7 before, /device:TPU:1 now
where the time goes in v3:
time: 72.4 us; the launch traced here: 71.9 us
  Pallas kernels  30.6 us (42%)
  starting transfers between devices  21.4 us (30%)
  waiting for transfers between devices  15.8 us (22%)
  other arithmetic  2.88 us (4%)
  local copies, waits for them, and re-layouts  0.9 us (1%)
    pallas_call x3, Pallas kernels, invert(): pl.pallas_call(functools.partial(band_kernel, base=base, stride=stride, t...  28.4 us
    ppermute x4, starting transfers between devices, shifted(): return lax.ppermute(value, 'acq', pairs)  11.9 us
    all_to_all x1, waiting for transfers between devices, program(): head = lax.all_to_all(sent[0], 'acq', 0, 0, tiled=True)  11 us
    all_to_all x1, starting transfers between devices, program(): head = lax.all_to_all(sent[0], 'acq', 0, 0, tiled=True)  5.78 us
    ppermute x4, waiting for transfers between devices, shifted(): return lax.ppermute(value, 'acq', pairs)  4.85 us
    all_to_all x1, starting transfers between devices, program(): tail = lax.all_to_all(sent[1], 'acq', 0, 0, tiled=True)  3.74 us
    pallas_call x1, Pallas kernels, order_tiles(): pl.pallas_call(functools.partial(order_kernel, spans=spans), in_specs=[pl...  2.27 us
  transfers between devices with their start and end apart: 6, of which 2 were waited for; matrix products, arithmetic and copies ran while one was open for 3% of the time, Pallas kernels for 27%

profile of v3, /device:TPU:1, one launch (start us, length us, event | category | flops | bytes accessed | tf_op | source)
XLA Modules:
  0.0 71.9 jit_solution(5693223336422291734)
XLA Ops:
  0.0 1.4 %multiply_convert_fusion.1 = (bf16[1,64,512]{2,1,0:T(8,128)(2,1)S(1)}, bf16[1,64,512]{2,1,0:T(8,128)(2,1)S(1)}) fusion(f32[1,64,512]{2,1,0:T(8,128)} %param.6), kind=kLoop, calls=%fused_computation.8 | loop fusion | flops 131072 | bytes 262144 | tf_op jit(solution)/shard_map/convert_element_type | solution.py:203
  1.4 1.9 %collective-permute-start.1 = (bf16[1,128,512]{2,1,0:T(8,128)(2,1)S(1)}, bf16[1,128,512]{2,1,0:T(8,128)(2,1)S(1)}, u32[]{:S(2)}, u32[]{:S(2)}) collective-permute-start(bf16[1,128,512]{2,1,0:T(8,128)(2,1)S(1)} %pad_maximum_fusion.5), channel_id=1, source_target_pairs={{1,0},{2,1},{3,2},{4,3},{5,4},{6,5},{7,6},{8,7},{9,8},{10,9},{11,1... | collective-permute-start | bytes 393224 | tf_op jit(solution)/shard_map/ppermute | solution.py:198
  3.3 4.5 %collective-permute-start = (bf16[1,128,512]{2,1,0:T(8,128)(2,1)S(1)}, bf16[1,128,512]{2,1,0:T(8,128)(2,1)S(1)}, u32[]{:S(2)}, u32[]{:S(2)}) collective-permute-start(bf16[1,128,512]{2,1,0:T(8,128)(2,1)S(1)} %pad_maximum_fusion.5), channel_id=1, source_target_pairs={{0,1},{1,2},{2,3},{3,4},{4,5},{5,6},{6,7},{7,8},{8,9},{9,10},{10,1... | collective-permute-start | bytes 393224 | tf_op jit(solution)/shard_map/ppermute | solution.py:198
  7.9 2.3 %order_tiles.1 = (bf16[128,1536]{1,0:T(8,128)(2,1)}, bf16[128,1536]{1,0:T(8,128)(2,1)}) custom-call(s32[16]{0:T(128)} %order_ref.1, bf16[4,2,12,16,256]{4,3,2,1,0:T(8,128)(2,1)} %bitcast.27), custom_call_target="tpu_custom_call" | custom-call | tf_op jit(solution)/shard_map/order_tiles/pallas_call | solution.py:48
  10.1 5.8 %all-to-all-start.1 = ((bf16[16,8,1536]{2,1,0:T(8,128)(2,1)}), bf16[16,8,1536]{2,1,0:T(8,128)(2,1)S(1)}, u32[]{:S(2)}, u32[]{:S(2)}) async-start(bf16[16,8,1536]{2,1,0:T(8,128)(2,1)} %bitcast.29), calls=%async_computation.1 | async-start | bytes 786432 | tf_op jit(solution)/shard_map/all_to_all | solution.py:227
  15.9 0.7 %add_select_fusion = s32[12,256]{1,0:T(8,128)S(1)} fusion(s32[12,256]{1,0:T(8,128)} %param.7), kind=kLoop, calls=%fused_computation.9 | loop fusion | flops 61440 | bytes 24576 | tf_op jit(solution)/shard_map/jit(floor_divide)/jit(_where)/select_n | solution.py:234
  16.7 0.0 collective-permute-done.1
  16.7 0.0 collective-permute-done
  16.8 11.0 %all-to-all-done.1 = bf16[16,8,1536]{2,1,0:T(8,128)(2,1)S(1)} async-done(((bf16[16,8,1536]{2,1,0:T(8,128)(2,1)}), bf16[16,8,1536]{2,1,0:T(8,128)(2,1)S(1)}, u32[]{:S(2)}, u32[]{:S(2)}) %all-to-all-start.1) | async-done | bytes 393248 | tf_op jit(solution)/shard_map/all_to_all | solution.py:227
  27.8 3.7 %all-to-all-start = ((bf16[16,8,1536]{2,1,0:T(8,128)(2,1)}), bf16[16,8,1536]{2,1,0:T(8,128)(2,1)S(1)}, u32[]{:S(2)}, u32[]{:S(2)}) async-start(bf16[16,8,1536]{2,1,0:T(8,128)(2,1)} %bitcast.28), calls=%async_computation | async-start | bytes 786432 | tf_op jit(solution)/shard_map/all_to_all | solution.py:228
  31.5 0.1 pad_maximum_fusion.2
  31.6 0.2 reshape.18
  31.7 0.1 reshape.19
  31.9 0.5 pad_maximum_fusion
  32.4 0.2 reshape.20
  32.6 3.5 %collective-permute-start.2 = (bf16[128,256]{1,0:T(8,128)(2,1)S(1)}, bf16[128,256]{1,0:T(8,128)(2,1)S(1)}, u32[]{:S(2)}, u32[]{:S(2)}) collective-permute-start(bf16[128,256]{1,0:T(8,128)(2,1)S(1)} %slice.66), channel_id=1, source_target_pairs={{0,1},{1,2},{2,3},{3,4},{4,5},{5,6},{6,7},{7,8},{8,9},{9,10},{10,1... | collective-permute-start | bytes 196616 | tf_op jit(solution)/shard_map/ppermute | solution.py:198
  36.2 1.9 %collective-permute-start.3 = (bf16[128,512]{1,0:T(8,128)(2,1)S(1)}, bf16[128,512]{1,0:T(8,128)(2,1)S(1)}, u32[]{:S(2)}, u32[]{:S(2)}) collective-permute-start(bf16[128,512]{1,0:T(8,128)(2,1)S(1)} %slice.67), channel_id=1, source_target_pairs={{1,0},{2,1},{3,2},{4,3},{5,4},{6,5},{7,6},{8,7},{9,8},{10,9},{11,1... | collective-permute-start | bytes 393224 | tf_op jit(solution)/shard_map/ppermute | solution.py:198
  38.1 0.1 broadcast_multiply_fusion.back_ref
  38.2 0.4 copy.14
  38.6 0.0 collective-permute-done.2
  38.6 4.8 %collective-permute-done.3 = bf16[128,512]{1,0:T(8,128)(2,1)S(1)} collective-permute-done((bf16[128,512]{1,0:T(8,128)(2,1)S(1)}, bf16[128,512]{1,0:T(8,128)(2,1)S(1)}, u32[]{:S(2)}, u32[]{:S(2)}) %collective-permute-start.3) | collective-permute-done | bytes 131104 | tf_op jit(solution)/shard_map/ppermute | solution.py:198
  43.5 10.9 %invert.3.refs_0_ = bf16[12,256,1024]{2,1,0:T(8,128)(2,1)} custom-call(bf16[128,1536]{1,0:T(8,128)(2,1)S(1)} %pad_maximum_fusion.4.target_ref, s32[2,1,256]{2,1,0:T(1,128)S(1)} %pad_add_fusion.1.run_ref, bf16[3,128,1024]{2,1,0:T(8,128)(2,1)S(1)} %broadcast_multiply_fusion.back_ref, bf16[3,1024,128]{2,1,0:T(8,128)(2,1)S(1)} %bitcast.18), custom_call_target="tpu_custom_call" | custom-call | tf_op jit(solution)/shard_map/invert/pallas_call | solution.py:168
  54.4 6.1 %invert.4.refs_0_ = bf16[12,256,1024]{2,1,0:T(8,128)(2,1)} custom-call(bf16[128,768]{1,0:T(8,128)(2,1)S(1)} %slice.64.target_ref, s32[1,1,256]{2,1,0:T(1,128)S(1)} %get-tuple-element.18.run_ref, bf16[3,128,1024]{2,1,0:T(8,128)(2,1)S(1)} %broadcast_multiply_fusion.back_ref, bf16[3,1024,128]{2,1,0:T(8,128)(2,1)S(1)} %bitcast.19, ...), custom_call_target="tpu_custom_call", output_to_operand_aliasing={{}: (4, {})} | custom-call | tf_op jit(solution)/shard_map/invert/pallas_call | solution.py:168
  60.6 0.0 all-to-all-done
  60.6 11.3 %invert.5 = bf16[12,256,1024]{2,1,0:T(8,128)(2,1)} custom-call(bf16[128,1536]{1,0:T(8,128)(2,1)S(1)} %bitcast.21, s32[2,1,256]{2,1,0:T(1,128)S(1)} %pad_add_fusion.run_ref, bf16[3,128,1024]{2,1,0:T(8,128)(2,1)S(1)} %broadcast_multiply_fusion.back_ref, bf16[3,1024,128]{2,1,0:T(8,128)(2,1)S(1)} %bitcast.20, ...), custom_call_target="tpu_custom_call", output_to_operand_aliasing={{}: (4, {})} | custom-call | tf_op jit(solution)/shard_map/invert/pallas_call | solution.py:168
  (10 shorter events, 0.2 us)
Async XLA Ops:
  1.4 15.3 %collective-permute-start.1 = (bf16[1,128,512]{2,1,0:T(8,128)(2,1)S(1)}, bf16[1,128,512]{2,1,0:T(8,128)(2,1)S(1)}, u32[]{:S(2)}, u32[]{:S(2)}) collective-permute-start(bf16[1,128,512]{2,1,0:T(8,128)(2,1)S(1)} %pad_maximum_fusion.5), channel_id=1, source_target_pairs={{1,0},{2,1},{3,2},{4,3},{5,4},{6,5},{7,6},{8,7},{9,8},{10,9},{11,1... | collective-permute-start | bytes 393224 | tf_op jit(solution)/shard_map/ppermute | solution.py:198
  3.3 13.4 %collective-permute-start = (bf16[1,128,512]{2,1,0:T(8,128)(2,1)S(1)}, bf16[1,128,512]{2,1,0:T(8,128)(2,1)S(1)}, u32[]{:S(2)}, u32[]{:S(2)}) collective-permute-start(bf16[1,128,512]{2,1,0:T(8,128)(2,1)S(1)} %pad_maximum_fusion.5), channel_id=1, source_target_pairs={{0,1},{1,2},{2,3},{3,4},{4,5},{5,6},{6,7},{7,8},{8,9},{9,10},{10,1... | collective-permute-start | bytes 393224 | tf_op jit(solution)/shard_map/ppermute | solution.py:198
  10.1 17.6 %all-to-all-start.1 = ((bf16[16,8,1536]{2,1,0:T(8,128)(2,1)}), bf16[16,8,1536]{2,1,0:T(8,128)(2,1)S(1)}, u32[]{:S(2)}, u32[]{:S(2)}) async-start(bf16[16,8,1536]{2,1,0:T(8,128)(2,1)} %bitcast.29), calls=%async_computation.1 | async-start | bytes 786432 | tf_op jit(solution)/shard_map/all_to_all | solution.py:227
  27.8 32.8 %all-to-all-start = ((bf16[16,8,1536]{2,1,0:T(8,128)(2,1)}), bf16[16,8,1536]{2,1,0:T(8,128)(2,1)S(1)}, u32[]{:S(2)}, u32[]{:S(2)}) async-start(bf16[16,8,1536]{2,1,0:T(8,128)(2,1)} %bitcast.28), calls=%async_computation | async-start | bytes 786432 | tf_op jit(solution)/shard_map/all_to_all | solution.py:228
  32.6 6.0 %collective-permute-start.2 = (bf16[128,256]{1,0:T(8,128)(2,1)S(1)}, bf16[128,256]{1,0:T(8,128)(2,1)S(1)}, u32[]{:S(2)}, u32[]{:S(2)}) collective-permute-start(bf16[128,256]{1,0:T(8,128)(2,1)S(1)} %slice.66), channel_id=1, source_target_pairs={{0,1},{1,2},{2,3},{3,4},{4,5},{5,6},{6,7},{7,8},{8,9},{9,10},{10,1... | collective-permute-start | bytes 196616 | tf_op jit(solution)/shard_map/ppermute | solution.py:198
  36.2 7.3 %collective-permute-start.3 = (bf16[128,512]{1,0:T(8,128)(2,1)S(1)}, bf16[128,512]{1,0:T(8,128)(2,1)S(1)}, u32[]{:S(2)}, u32[]{:S(2)}) collective-permute-start(bf16[128,512]{1,0:T(8,128)(2,1)S(1)} %slice.67), channel_id=1, source_target_pairs={{1,0},{2,1},{3,2},{4,3},{5,4},{6,5},{7,6},{8,7},{9,8},{10,9},{11,1... | collective-permute-start | bytes 393224 | tf_op jit(solution)/shard_map/ppermute | solution.py:198

commit v4 on v3

v4 whole, which is shorter than its diff:
```python
import functools
import math

import jax
import jax.numpy as jnp
from jax import lax
from jax.experimental import pallas as pl
from jax.experimental.pallas import tpu as pltpu
from jax.sharding import PartitionSpec as P


ITERS = 3
BAND = 3
STEP_SIZE = 0.0625
SHRINK_LEVEL = 3.0


def dot(a, b, dims=((1,), (0,))):
    return lax.dot_general(a, b, (dims, ((), ())), preferred_element_type=jnp.float32)


def order_kernel(order_ref, *refs, spans, ahead_rows):
    stack_ref, sent_refs = refs[0], refs[1:]
    acqs, parts, _, tiles, columns = stack_ref.shape
    lines = acqs * parts * tiles
    share = acqs * parts
    target = lax.broadcasted_iota(jnp.int32, (lines, 1), 0)
    source = lax.broadcasted_iota(jnp.int32, (1, lines), 1)
    block = lax.rem(source, tiles)
    part = lax.rem(lax.div(source, tiles), parts)
    acq = lax.div(source, tiles * parts)
    tile = jnp.zeros((1, lines), jnp.int32)
    for k in range(tiles):
        tile = jnp.where(block == k, order_ref[k], tile)
    after = jnp.where(tile == tiles - 1, 0, tile + 1)
    inner = part * acqs + acq
    pick = jnp.where(target == tile * share + inner, 1.0, 0.0).astype(jnp.bfloat16)
    pick_after = jnp.where(target == after * share + inner, 1.0, 0.0).astype(jnp.bfloat16)
    for sent_ref, span in zip(sent_refs, spans):
        for q, row in enumerate(span):
            lump = stack_ref[:, :, row].reshape(lines, columns)
            chosen = pick_after if row in ahead_rows else pick
            sent_ref[:, q * columns : (q + 1) * columns] = dot(chosen, lump).astype(sent_ref.dtype)


def order_tiles(measurements, tile_order, spans, ahead_rows):
    acqs, parts, tiles, _, columns = measurements.shape
    stack = measurements.transpose(0, 1, 3, 2, 4)
    lines = acqs * parts * tiles
    whole = pl.BlockSpec(memory_space=pltpu.VMEM)
    return pl.pallas_call(
        functools.partial(order_kernel, spans=spans, ahead_rows=ahead_rows),
        in_specs=[pl.BlockSpec(memory_space=pltpu.SMEM), whole],
        out_specs=[whole] * len(spans),
        out_shape=[
            jax.ShapeDtypeStruct((lines, len(span) * columns), measurements.dtype) for span in spans
        ],
        name="order_tiles",
    )(tile_order, stack)


def run_sums(energy, pick):
    return dot(pick, energy.astype(jnp.bfloat16))


def shrink_factor(sums, pick):
    factor = jnp.maximum(1.0 - SHRINK_LEVEL * lax.rsqrt(jnp.maximum(sums, SHRINK_LEVEL**2)), 0.0)
    high = factor.astype(jnp.bfloat16)
    low = (factor - high.astype(jnp.float32)).astype(jnp.bfloat16)
    both = jnp.concatenate([high, low], axis=0)
    return dot(jnp.concatenate([pick, pick], axis=0), both, ((0,), (0,)))


def band_kernel(joined_ref, target_ref, run_ref, back_ref, ahead_ref, *refs, edge, base, held, late):
    refs = list(refs)
    if held:
        refs.pop(0)
    late_ref = refs.pop(0) if late else None
    out_ref = refs.pop(0)
    above_ref = refs.pop(0) if edge else None
    target_sc, resid_sc, step_sc, energy_sc, factor_sc, image_sc, sem = refs
    step = pl.program_id(0)
    steps = pl.num_programs(0)
    columns = run_ref.shape[2]
    elevations = factor_sc.shape[2]
    tile_width = energy_sc.shape[2]
    groups = -(-(columns // BAND + 2) // 16) * 16
    weight_of = (0 if edge else 1,) + (1,) * (BAND - 1)
    set_of = weight_of
    span = [slice(q * columns, (q + 1) * columns) for q in range(BAND)]

    def copies(of):
        first = BAND * (base + of) - 1
        targets = [above_ref if edge and q == 0 else out_ref.at[first + q] for q in range(BAND)]
        pairs = [pltpu.make_async_copy(image_sc.at[q], targets[q], sem.at[q]) for q in range(BAND)]
        if late:
            pairs.append(pltpu.make_async_copy(late_ref, out_ref.at[out_ref.shape[0] - 1], sem.at[BAND]))
        return pairs

    group = lax.broadcasted_iota(jnp.int32, (groups, columns), 0)
    picks = [
        jnp.where(group == run_ref[0, n : n + 1], 1.0, 0.0).astype(jnp.bfloat16)
        for n in range(run_ref.shape[1])
    ]
    target_sc[...] = target_ref[...].astype(jnp.float32).T

    def descend(is_first):
        for at in range(0, elevations, tile_width):
            real = slice(at, at + tile_width)
            imag = slice(elevations + at, elevations + at + tile_width)
            for q in range(BAND):
                if is_first:
                    resid = target_sc[span[q]].astype(jnp.bfloat16)
                else:
                    resid = resid_sc[span[q]]
                step_real = dot(resid, back_ref[weight_of[q], :, real])
                step_imag = dot(resid, back_ref[weight_of[q], :, imag])
                if not is_first:
                    factor = factor_sc[set_of[q], :, real]
                    step_real += step_sc[span[q], real] * factor
                    step_imag += step_sc[span[q], imag] * factor
                step_sc[span[q], real] = step_real
                step_sc[span[q], imag] = step_imag
                energy = step_real * step_real + step_imag * step_imag
                if q > 0 and set_of[q] == set_of[q - 1]:
                    energy += energy_sc[set_of[q]]
                if q < BAND - 1:
                    energy_sc[set_of[q]] = energy
            sums = run_sums(energy, picks[-1])
            if edge:
                apart = run_sums(energy_sc[0], picks[0])
                joined = joined_ref[0] > 0
                factor_sc[0, :, real] = shrink_factor(
                    jnp.where(joined, apart + sums, apart), picks[0]
                )
                sums = jnp.where(joined, apart + sums, sums)
            factor_sc[1, :, real] = shrink_factor(sums, picks[-1])

    def predict():
        for q in range(BAND):
            guess = jnp.zeros((columns, target_sc.shape[1]), jnp.float32)
            for half in range(2):
                part = slice(half * elevations, (half + 1) * elevations)
                rounded = (step_sc[span[q], part] * factor_sc[set_of[q]]).astype(jnp.bfloat16)
                guess += dot(rounded, ahead_ref[weight_of[q], part])
            resid_sc[span[q]] = (target_sc[span[q]] - guess).astype(jnp.bfloat16)

    descend(True)

    @pl.loop(1, ITERS)
    def _(i):
        predict()
        descend(False)

    @pl.when(step > 0)
    def _():
        for copy in copies(step - 1)[:BAND]:
            copy.wait()

    for q in range(BAND):
        for half in range(2):
            part = slice(half * elevations, (half + 1) * elevations)
            image_sc[q, :, part] = (step_sc[span[q], part] * factor_sc[set_of[q]]).astype(
                image_sc.dtype
            )
        copies(step)[q].start()

    @pl.when(step == steps - 1)
    def _():
        if late:
            copies(step)[BAND].start()
        for copy in copies(step):
            copy.wait()


def invert(joined, targets, runs, back, ahead, out_shape, *, offset, base, edge=False, out=None, late=None):
    lines = targets.shape[0]
    steps, kinds, columns = runs.shape
    elevations = back.shape[2] // 2
    whole = pl.BlockSpec(memory_space=pltpu.VMEM)
    far = pl.BlockSpec(memory_space=pl.ANY)
    pixels = BAND * columns
    tile_width = 256
    shape = jax.ShapeDtypeStruct(out_shape, jnp.bfloat16)
    above = jax.ShapeDtypeStruct(out_shape[1:], jnp.bfloat16)
    extra = ([] if out is None else [out]) + ([] if late is None else [late])
    extra_specs = ([] if out is None else [far]) + ([] if late is None else [whole])
    return pl.pallas_call(
        functools.partial(
            band_kernel, edge=edge, base=base, held=out is not None, late=late is not None
        ),
        grid=(steps,),
        in_specs=[
            pl.BlockSpec(memory_space=pltpu.SMEM),
            pl.BlockSpec((lines, pixels), lambda i: (0, i + offset)),
            pl.BlockSpec((1, kinds, columns), lambda i: (i, 0, 0)),
            whole,
            whole,
        ]
        + extra_specs,
        out_specs=[far, far] if edge else far,
        out_shape=[shape, above] if edge else shape,
        input_output_aliases={} if out is None else {5: 0},
        scratch_shapes=[
            pltpu.VMEM((pixels, lines), jnp.float32),
            pltpu.VMEM((pixels, lines), jnp.bfloat16),
            pltpu.VMEM((pixels, 2 * elevations), jnp.float32),
            pltpu.VMEM((2, columns, tile_width), jnp.float32),
            pltpu.VMEM((2, columns, elevations), jnp.float32),
            pltpu.VMEM((BAND, columns, 2 * elevations), jnp.bfloat16),
            pltpu.SemaphoreType.DMA((BAND + 1,)),
        ],
        compiler_params=pltpu.CompilerParams(vmem_limit_bytes=40 * 1024 * 1024),
        name="invert_edge" if edge else "invert",
    )(joined, targets, runs, back, ahead, *extra)


def turned(value, step):
    count = lax.axis_size("acq")
    return lax.ppermute(value, "acq", [(i, (i + step) % count) for i in range(count)])


def steering_of(phase):
    scale = 1.0 / math.sqrt(phase.shape[1])
    real = (jnp.cos(phase) * scale).astype(jnp.bfloat16)
    imag = (jnp.sin(phase) * scale).astype(jnp.bfloat16)
    return jnp.concatenate([real, imag], axis=1)


def planes_of(steering, acqs):
    count, lines, elevations = steering.shape
    real, imag = steering[:, : lines // 2], steering[:, lines // 2 :]
    upper = jnp.concatenate([real, -imag], axis=2).reshape(count, -1, 1, acqs, 2 * elevations)
    lower = jnp.concatenate([imag, real], axis=2).reshape(count, -1, 1, acqs, 2 * elevations)
    return jnp.concatenate([upper, lower], axis=2).reshape(count, lines, 2 * elevations)


def program(measurements, tile_order, steer_phase, group_ids):
    acqs = measurements.shape[0]
    rows, columns = group_ids.shape
    elevations = steer_phase.shape[2]
    assert rows % BAND == 0
    bands = rows // BAND
    edge = [rows - 1] + list(range(BAND - 1))
    inner = [list(range(BAND * b - 1, BAND * b + 2)) for b in range(1, bands)]
    early = 1
    spans = [edge + sum(inner[:early], []), sum(inner[early:], [])]
    sent = order_tiles(measurements, tile_order, spans, (rows - 1,))
    head = lax.all_to_all(sent[0], "acq", 0, 0, tiled=True)
    tail = lax.all_to_all(sent[1], "acq", 0, 0, tiled=True)
    mine = steering_of(steer_phase)
    steering = jnp.concatenate([turned(mine, 1), mine], axis=0)
    back = planes_of(steering, acqs)
    ahead = back.transpose(0, 2, 1)
    back = back * STEP_SIZE
    runs = (group_ids % columns + BAND - 1) // BAND
    first = lax.axis_index("acq") == 0
    column = jnp.arange(columns, dtype=jnp.int32)
    turn = (columns - 1) % BAND
    last_starts = jnp.maximum(0, BAND * ((column - turn + BAND) // BAND) - BAND + turn)
    last_runs = (last_starts + BAND - 1) // BAND
    edge_runs = jnp.stack([jnp.where(first, last_runs, runs[0]), runs[0]])[None]
    inner_runs = runs[BAND - 1 : rows - 1 : BAND][:, None]
    joined = jnp.where(first, 0, 1).reshape(1)
    shape = (rows, columns, 2 * elevations)
    out, above = invert(joined, head, edge_runs, back, ahead, shape, offset=0, base=0, edge=True)
    late = turned(above, -1)
    out = invert(joined, head, inner_runs[:early], back, ahead, shape, offset=1, base=1, out=out)
    return invert(
        joined, tail, inner_runs[early:], back, ahead, shape,
        offset=0, base=1 + early, out=out, late=late,
    )


def solution(mesh):
    placed = (
        P(("groups", "acq"), None, None, None, None),
        P("groups"),
        P(("groups", "acq"), None, None),
        P(("groups", "acq"), None),
    )
    return jax.shard_map(
        program,
        mesh=mesh,
        in_specs=placed,
        out_specs=P(("groups", "acq"), None, None),
        check_vma=False,
    )
```

time: 72.4 us -> 56.8 us (0.78)
  the two profiles are of different devices: /device:TPU:1 before, /device:TPU:0 now
where the time goes in v4:
time: 56.8 us; the launch traced here: 56.4 us
  Pallas kernels  26.4 us (46%)
  starting transfers between devices  15.7 us (28%)
  waiting for transfers between devices  9.84 us (17%)
  other arithmetic  3.12 us (5%)
  local copies, waits for them, and re-layouts  1.14 us (2%)
    pallas_call x3, Pallas kernels, invert(): pl.pallas_call(functools.partial(band_kernel, edge=edge, base=base, held=...  24.2 us
    all_to_all x1, waiting for transfers between devices, program(): head = lax.all_to_all(sent[0], 'acq', 0, 0, tiled=True)  9.42 us
    all_to_all x1, starting transfers between devices, program(): head = lax.all_to_all(sent[0], 'acq', 0, 0, tiled=True)  7.21 us
    ppermute x2, starting transfers between devices, turned(): lax.ppermute(value, 'acq', [(i, (i + step) % count) for i in range(count)])  4.92 us
    all_to_all x1, starting transfers between devices, program(): tail = lax.all_to_all(sent[1], 'acq', 0, 0, tiled=True)  3.55 us
    pallas_call x1, Pallas kernels, order_tiles(): pl.pallas_call(functools.partial(order_kernel, spans=spans, ahead_rows=ah...  2.27 us
    convert_element_type x1, other arithmetic, steering_of(): real = (jnp.cos(phase) * scale).astype(jnp.bfloat16)  1.37 us
  transfers between devices with their start and end apart: 4, of which 2 were waited for; matrix products, arithmetic and copies ran while one was open for 5% of the time, Pallas kernels for 26%

profile of v4, /device:TPU:0, one launch (start us, length us, event | category | flops | bytes accessed | tf_op | source)
XLA Modules:
  0.0 56.4 jit_solution(4439036230572411898)
XLA Ops:
  0.0 1.4 %multiply_convert_fusion.1 = (bf16[1,64,512]{2,1,0:T(8,128)(2,1)S(1)}, bf16[1,64,512]{2,1,0:T(8,128)(2,1)S(1)}) fusion(f32[1,64,512]{2,1,0:T(8,128)} %param.6), kind=kLoop, calls=%fused_computation.7 | loop fusion | flops 131072 | bytes 262144 | tf_op jit(solution)/shard_map/convert_element_type | solution.py:225
  1.4 0.5 collective-permute-start
  1.9 2.3 %order_tiles.1 = (bf16[128,1536]{1,0:T(8,128)(2,1)}, bf16[128,1536]{1,0:T(8,128)(2,1)}) custom-call(s32[16]{0:T(128)} %order_ref.1, bf16[4,2,12,16,256]{4,3,2,1,0:T(8,128)(2,1)} %bitcast.24), custom_call_target="tpu_custom_call" | custom-call | tf_op jit(solution)/shard_map/order_tiles/pallas_call | solution.py:51
  4.2 7.2 %all-to-all-start.1 = ((bf16[16,8,1536]{2,1,0:T(8,128)(2,1)}), bf16[16,8,1536]{2,1,0:T(8,128)(2,1)S(1)}, u32[]{:S(2)}, u32[]{:S(2)}) async-start(bf16[16,8,1536]{2,1,0:T(8,128)(2,1)} %bitcast.26), calls=%async_computation.1 | async-start | bytes 786432 | tf_op jit(solution)/shard_map/all_to_all | solution.py:249
  11.4 0.7 %add_select_fusion = s32[12,256]{1,0:T(8,128)S(1)} fusion(s32[12,256]{1,0:T(8,128)} %param.7), kind=kLoop, calls=%fused_computation.8 | loop fusion | flops 61440 | bytes 24576 | tf_op jit(solution)/shard_map/jit(floor_divide)/jit(_where)/select_n | solution.py:256
  12.2 0.0 collective-permute-done
  12.3 0.3 copy.16
  12.6 0.3 copy.17
  12.9 0.7 %pad_maximum_fusion = bf16[2,16,2,4,1024]{4,0,3,2,1:T(2,128)(2,1)S(1)} fusion(bf16[2,16,1,4,1024]{4,0,3,2,1:T(2,128)(2,1)S(1)} %bitcast.23, bf16[2,16,1,4,1024]{4,0,3,2,1:T(2,128)(2,1)S(1)} %bitcast.22), kind=kLoop, calls=%fused_computation | loop fusion | flops 262144 | bytes 1048576 | tf_op jit(solution)/shard_map/concatenate | solution.py:235
  13.6 0.6 %copy.15 = bf16[2,128,1024]{1,2,0:T(8,128)(2,1)S(1)} copy(bf16[2,128,1024]{2,0,1:T(2,128)(2,1)S(1)} %bitcast.20) | data formatting | bytes 1048576 | tf_op jit(solution)/shard_map/reshape | solution.py:235
  14.2 9.4 %all-to-all-done.1 = bf16[16,8,1536]{2,1,0:T(8,128)(2,1)S(1)} async-done(((bf16[16,8,1536]{2,1,0:T(8,128)(2,1)}), bf16[16,8,1536]{2,1,0:T(8,128)(2,1)S(1)}, u32[]{:S(2)}, u32[]{:S(2)}) %all-to-all-start.1) | async-done | bytes 393248 | tf_op jit(solution)/shard_map/all_to_all | solution.py:249
  23.6 3.6 %all-to-all-start = ((bf16[16,8,1536]{2,1,0:T(8,128)(2,1)}), bf16[16,8,1536]{2,1,0:T(8,128)(2,1)S(1)}, u32[]{:S(2)}, u32[]{:S(2)}) async-start(bf16[16,8,1536]{2,1,0:T(8,128)(2,1)} %bitcast.25), calls=%async_computation | async-start | bytes 786432 | tf_op jit(solution)/shard_map/all_to_all | solution.py:250
  27.1 0.2 copy_multiply_fusion.back_ref
  27.3 6.3 %invert_edge.1 = (bf16[12,256,1024]{2,1,0:T(8,128)(2,1)}, bf16[256,1024]{1,0:T(8,128)(2,1)S(1)}) custom-call(s32[1]{0:T(128)} %bitcast.joined_ref, bf16[128,1536]{1,0:T(8,128)(2,1)S(1)} %bitcast.17, s32[1,2,256]{2,1,0:T(2,128)S(1)} %add_bitcast_fusion.run_ref, bf16[2,128,1024]{2,1,0:T(8,128)(2,1)S(1)} %copy_multiply_fusion.back_ref, ...), custom_call_target="tpu_custom_call" | custom-call | tf_op jit(solution)/shard_map/invert_edge/pallas_call | solution.py:188
  33.6 4.4 %collective-permute-start.1 = (bf16[256,1024]{1,0:T(8,128)(2,1)S(1)}, bf16[256,1024]{1,0:T(8,128)(2,1)S(1)}, u32[]{:S(2)}, u32[]{:S(2)}) collective-permute-start(bf16[256,1024]{1,0:T(8,128)(2,1)S(1)} %get-tuple-element.12), channel_id=1, source_target_pairs={{0,15},{1,0},{2,1},{3,2},{4,3},{5,4},{6,5},{7,6},{8,7},{9,8},{10,9... | collective-permute-start | bytes 1572872 | tf_op jit(solution)/shard_map/ppermute | solution.py:220
  38.0 6.2 %invert.2.refs_0_ = bf16[12,256,1024]{2,1,0:T(8,128)(2,1)} custom-call(s32[1]{0:T(128)} %bitcast.joined_ref, bf16[128,1536]{1,0:T(8,128)(2,1)S(1)} %bitcast.18, s32[1,1,256]{2,1,0:T(1,128)S(1)} %slice_bitcast_fusion.run_ref, bf16[2,128,1024]{2,1,0:T(8,128)(2,1)S(1)} %copy_multiply_fusion.back_ref, ...), custom_call_target="tpu_custom_call", output_to_operand_aliasing={{}: (5, {})} | custom-call | tf_op jit(solution)/shard_map/invert/pallas_call | solution.py:188
  44.3 0.0 all-to-all-done
  44.3 0.4 collective-permute-done.1.refs_1_
  44.7 11.7 %invert.3 = bf16[12,256,1024]{2,1,0:T(8,128)(2,1)} custom-call(s32[1]{0:T(128)} %bitcast.joined_ref, bf16[128,1536]{1,0:T(8,128)(2,1)S(1)} %bitcast.19, s32[2,1,256]{2,1,0:T(1,128)S(1)} %slice.27.run_ref, bf16[2,128,1024]{2,1,0:T(8,128)(2,1)S(1)} %copy_multiply_fusion.back_ref, bf16[2,1024,128]{2,1,0:T(8,128)(2,1)S(1)} %bitcast.16, ...), custom_call_target="tpu_custom_call", output_to_operand_aliasing={{}: (5, {})} | custom-call | tf_op jit(solution)/shard_map/invert/pallas_call | solution.py:188
  (10 shorter events, 0.2 us)
Async XLA Ops:
  1.4 10.8 %collective-permute-start = (bf16[1,128,512]{2,1,0:T(8,128)(2,1)S(1)}, bf16[1,128,512]{2,1,0:T(8,128)(2,1)S(1)}, u32[]{:S(2)}, u32[]{:S(2)}) collective-permute-start(bf16[1,128,512]{2,1,0:T(8,128)(2,1)S(1)} %pad_maximum_fusion.3), channel_id=1, source_target_pairs={{0,1},{1,2},{2,3},{3,4},{4,5},{5,6},{6,7},{7,8},{8,9},{9,10},{10,1... | collective-permute-start | bytes 393224 | tf_op jit(solution)/shard_map/ppermute | solution.py:220
  4.2 19.4 %all-to-all-start.1 = ((bf16[16,8,1536]{2,1,0:T(8,128)(2,1)}), bf16[16,8,1536]{2,1,0:T(8,128)(2,1)S(1)}, u32[]{:S(2)}, u32[]{:S(2)}) async-start(bf16[16,8,1536]{2,1,0:T(8,128)(2,1)} %bitcast.26), calls=%async_computation.1 | async-start | bytes 786432 | tf_op jit(solution)/shard_map/all_to_all | solution.py:249
  23.6 20.7 %all-to-all-start = ((bf16[16,8,1536]{2,1,0:T(8,128)(2,1)}), bf16[16,8,1536]{2,1,0:T(8,128)(2,1)S(1)}, u32[]{:S(2)}, u32[]{:S(2)}) async-start(bf16[16,8,1536]{2,1,0:T(8,128)(2,1)} %bitcast.25), calls=%async_computation | async-start | bytes 786432 | tf_op jit(solution)/shard_map/all_to_all | solution.py:250
  33.6 11.1 %collective-permute-start.1 = (bf16[256,1024]{1,0:T(8,128)(2,1)S(1)}, bf16[256,1024]{1,0:T(8,128)(2,1)S(1)}, u32[]{:S(2)}, u32[]{:S(2)}) collective-permute-start(bf16[256,1024]{1,0:T(8,128)(2,1)S(1)} %get-tuple-element.12), channel_id=1, source_target_pairs={{0,15},{1,0},{2,1},{3,2},{4,3},{5,4},{6,5},{7,6},{8,7},{9,8},{10,9... | collective-permute-start | bytes 1572872 | tf_op jit(solution)/shard_map/ppermute | solution.py:220

commit v5 on v4

--- a/solution.py
+++ b/solution.py
@@ -122,13 +122,17 @@
                 step_sc[span[q], real] = step_real
                 step_sc[span[q], imag] = step_imag
                 energy = step_real * step_real + step_imag * step_imag
+                slot = 2 * (at // tile_width) + set_of[q]
                 if q > 0 and set_of[q] == set_of[q - 1]:
-                    energy += energy_sc[set_of[q]]
-                if q < BAND - 1:
-                    energy_sc[set_of[q]] = energy
-            sums = run_sums(energy, picks[-1])
+                    energy += energy_sc[slot]
+                energy_sc[slot] = energy
+
+        for at in range(0, elevations, tile_width):
+            real = slice(at, at + tile_width)
+            slot = 2 * (at // tile_width)
+            sums = run_sums(energy_sc[slot + 1], picks[-1])
             if edge:
-                apart = run_sums(energy_sc[0], picks[0])
+                apart = run_sums(energy_sc[slot], picks[0])
                 joined = joined_ref[0] > 0
                 factor_sc[0, :, real] = shrink_factor(
                     jnp.where(joined, apart + sums, apart), picks[0]
@@ -205,7 +209,7 @@
             pltpu.VMEM((pixels, lines), jnp.float32),
             pltpu.VMEM((pixels, lines), jnp.bfloat16),
             pltpu.VMEM((pixels, 2 * elevations), jnp.float32),
-            pltpu.VMEM((2, columns, tile_width), jnp.float32),
+            pltpu.VMEM((2 * (elevations // tile_width), columns, tile_width), jnp.float32),
             pltpu.VMEM((2, columns, elevations), jnp.float32),
             pltpu.VMEM((BAND, columns, 2 * elevations), jnp.bfloat16),
             pltpu.SemaphoreType.DMA((BAND + 1,)),
@@ -249,8 +253,8 @@
     head = lax.all_to_all(sent[0], "acq", 0, 0, tiled=True)
     tail = lax.all_to_all(sent[1], "acq", 0, 0, tiled=True)
     mine = steering_of(steer_phase)
-    steering = jnp.concatenate([turned(mine, 1), mine], axis=0)
-    back = planes_of(steering, acqs)
+    before = turned(mine, 1)
+    back = planes_of(jnp.concatenate([before, mine], axis=0), acqs)
     ahead = back.transpose(0, 2, 1)
     back = back * STEP_SIZE
     runs = (group_ids % columns + BAND - 1) // BAND
@@ -266,9 +270,13 @@
     out, above = invert(joined, head, edge_runs, back, ahead, shape, offset=0, base=0, edge=True)
     late = turned(above, -1)
     out = invert(joined, head, inner_runs[:early], back, ahead, shape, offset=1, base=1, out=out)
+    out = invert(
+        joined, tail, inner_runs[early:-1], back, ahead, shape,
+        offset=0, base=1 + early, out=out,
+    )
     return invert(
-        joined, tail, inner_runs[early:], back, ahead, shape,
-        offset=0, base=1 + early, out=out, late=late,
+        joined, tail, inner_runs[-1:], back, ahead, shape,
+        offset=bands - 2 - early, base=bands - 1, out=out, late=late,
     )
 
 

time: 56.8 us -> 54.1 us (0.952)
  Pallas kernels: 26.4 us -> 23.9 us
    pallas_call x3 -> x4, Pallas kernels: 24.2 us -> 21.6 us  [invert(): pl.pallas_call(functools.partial(band_kernel, edge=edge, base=base, held=...]
  transfers between devices with their start and end apart: 4 -> 4, of which waited for: 2 -> 1; matrix products, arithmetic and copies ran while one was open for 5% -> 5% of each run, Pallas kernels for 26% -> 34%
where the time goes in v5:
time: 54.1 us; the launch traced here: 53.7 us
  Pallas kernels  23.9 us (44%)
  starting transfers between devices  15.8 us (29%)
  waiting for transfers between devices  9.42 us (17%)
  other arithmetic  3.12 us (6%)
  local copies, waits for them, and re-layouts  1.14 us (2%)
    pallas_call x4, Pallas kernels, invert(): pl.pallas_call(functools.partial(band_kernel, edge=edge, base=base, held=...  21.6 us
    all_to_all x1, waiting for transfers between devices, program(): head = lax.all_to_all(sent[0], 'acq', 0, 0, tiled=True)  9.42 us
    all_to_all x1, starting transfers between devices, program(): head = lax.all_to_all(sent[0], 'acq', 0, 0, tiled=True)  7.21 us
    ppermute x2, starting transfers between devices, turned(): lax.ppermute(value, 'acq', [(i, (i + step) % count) for i in range(count)])  5.09 us
    all_to_all x1, starting transfers between devices, program(): tail = lax.all_to_all(sent[1], 'acq', 0, 0, tiled=True)  3.55 us
    pallas_call x1, Pallas kernels, order_tiles(): pl.pallas_call(functools.partial(order_kernel, spans=spans, ahead_rows=ah...  2.27 us
    convert_element_type x1, other arithmetic, steering_of(): real = (jnp.cos(phase) * scale).astype(jnp.bfloat16)  1.37 us
  transfers between devices with their start and end apart: 4, of which 1 were waited for; matrix products, arithmetic and copies ran while one was open for 5% of the time, Pallas kernels for 34%

profile of v5, /device:TPU:0, one launch (start us, length us, event | category | flops | bytes accessed | tf_op | source)
XLA Modules:
  0.0 53.7 jit_solution(13965981276270909734)
XLA Ops:
  0.0 1.4 %multiply_convert_fusion.1 = (bf16[1,64,512]{2,1,0:T(8,128)(2,1)S(1)}, bf16[1,64,512]{2,1,0:T(8,128)(2,1)S(1)}) fusion(f32[1,64,512]{2,1,0:T(8,128)} %param.6), kind=kLoop, calls=%fused_computation.7 | loop fusion | flops 131072 | bytes 262144 | tf_op jit(solution)/shard_map/convert_element_type | solution.py:229
  1.4 0.5 %collective-permute-start = (bf16[1,128,512]{2,1,0:T(8,128)(2,1)S(1)}, bf16[1,128,512]{2,1,0:T(8,128)(2,1)S(1)}, u32[]{:S(2)}, u32[]{:S(2)}) collective-permute-start(bf16[1,128,512]{2,1,0:T(8,128)(2,1)S(1)} %pad_maximum_fusion.3), channel_id=1, source_target_pairs={{0,1},{1,2},{2,3},{3,4},{4,5},{5,6},{6,7},{7,8},{8,9},{9,10},{10,1... | collective-permute-start | bytes 393224 | tf_op jit(solution)/shard_map/ppermute | solution.py:224
  1.9 2.3 %order_tiles.1 = (bf16[128,1536]{1,0:T(8,128)(2,1)}, bf16[128,1536]{1,0:T(8,128)(2,1)}) custom-call(s32[16]{0:T(128)} %order_ref.1, bf16[4,2,12,16,256]{4,3,2,1,0:T(8,128)(2,1)} %bitcast.30), custom_call_target="tpu_custom_call" | custom-call | tf_op jit(solution)/shard_map/order_tiles/pallas_call | solution.py:51
  4.2 7.2 %all-to-all-start.1 = ((bf16[16,8,1536]{2,1,0:T(8,128)(2,1)}), bf16[16,8,1536]{2,1,0:T(8,128)(2,1)S(1)}, u32[]{:S(2)}, u32[]{:S(2)}) async-start(bf16[16,8,1536]{2,1,0:T(8,128)(2,1)} %bitcast.32), calls=%async_computation.1 | async-start | bytes 786432 | tf_op jit(solution)/shard_map/all_to_all | solution.py:253
  11.4 0.7 %add_select_fusion = s32[12,256]{1,0:T(8,128)S(1)} fusion(s32[12,256]{1,0:T(8,128)} %param.7), kind=kLoop, calls=%fused_computation.8 | loop fusion | flops 61440 | bytes 24576 | tf_op jit(solution)/shard_map/jit(floor_divide)/jit(_where)/select_n | solution.py:260
  12.2 0.0 collective-permute-done
  12.3 0.3 copy.18
  12.6 0.3 copy.19
  12.9 0.7 %pad_maximum_fusion = bf16[2,16,2,4,1024]{4,0,3,2,1:T(2,128)(2,1)S(1)} fusion(bf16[2,16,1,4,1024]{4,0,3,2,1:T(2,128)(2,1)S(1)} %bitcast.29, bf16[2,16,1,4,1024]{4,0,3,2,1:T(2,128)(2,1)S(1)} %bitcast.28), kind=kLoop, calls=%fused_computation | loop fusion | flops 262144 | bytes 1048576 | tf_op jit(solution)/shard_map/concatenate | solution.py:239
  13.6 0.6 %copy.17 = bf16[2,128,1024]{1,2,0:T(8,128)(2,1)S(1)} copy(bf16[2,128,1024]{2,0,1:T(2,128)(2,1)S(1)} %bitcast.26) | data formatting | bytes 1048576 | tf_op jit(solution)/shard_map/reshape | solution.py:239
  14.2 9.4 %all-to-all-done.1 = bf16[16,8,1536]{2,1,0:T(8,128)(2,1)S(1)} async-done(((bf16[16,8,1536]{2,1,0:T(8,128)(2,1)}), bf16[16,8,1536]{2,1,0:T(8,128)(2,1)S(1)}, u32[]{:S(2)}, u32[]{:S(2)}) %all-to-all-start.1) | async-done | bytes 393248 | tf_op jit(solution)/shard_map/all_to_all | solution.py:253
  23.6 3.6 %all-to-all-start = ((bf16[16,8,1536]{2,1,0:T(8,128)(2,1)}), bf16[16,8,1536]{2,1,0:T(8,128)(2,1)S(1)}, u32[]{:S(2)}, u32[]{:S(2)}) async-start(bf16[16,8,1536]{2,1,0:T(8,128)(2,1)} %bitcast.31), calls=%async_computation | async-start | bytes 786432 | tf_op jit(solution)/shard_map/all_to_all | solution.py:254
  27.1 0.2 copy_multiply_fusion.back_ref
  27.3 5.8 %invert_edge.1 = (bf16[12,256,1024]{2,1,0:T(8,128)(2,1)}, bf16[256,1024]{1,0:T(8,128)(2,1)S(1)}) custom-call(s32[1]{0:T(128)} %bitcast.joined_ref, bf16[128,1536]{1,0:T(8,128)(2,1)S(1)} %bitcast.22, s32[1,2,256]{2,1,0:T(2,128)S(1)} %add_bitcast_fusion.run_ref, bf16[2,128,1024]{2,1,0:T(8,128)(2,1)S(1)} %copy_multiply_fusion.back_ref, ...), custom_call_target="tpu_custom_call" | custom-call | tf_op jit(solution)/shard_map/invert_edge/pallas_call | solution.py:192
  33.1 4.5 %collective-permute-start.1 = (bf16[256,1024]{1,0:T(8,128)(2,1)S(1)}, bf16[256,1024]{1,0:T(8,128)(2,1)S(1)}, u32[]{:S(2)}, u32[]{:S(2)}) collective-permute-start(bf16[256,1024]{1,0:T(8,128)(2,1)S(1)} %get-tuple-element.12), channel_id=1, source_target_pairs={{0,15},{1,0},{2,1},{3,2},{4,3},{5,4},{6,5},{7,6},{8,7},{9,8},{10,9... | collective-permute-start | bytes 1572872 | tf_op jit(solution)/shard_map/ppermute | solution.py:224
  37.7 5.2 %invert.3.refs_0_ = bf16[12,256,1024]{2,1,0:T(8,128)(2,1)} custom-call(s32[1]{0:T(128)} %bitcast.joined_ref, bf16[128,1536]{1,0:T(8,128)(2,1)S(1)} %bitcast.23, s32[1,1,256]{2,1,0:T(1,128)S(1)} %get-tuple-element.22.run_ref, bf16[2,128,1024]{2,1,0:T(8,128)(2,1)S(1)} %copy_multiply_fusion.back_ref, ...), custom_call_target="tpu_custom_call", output_to_operand_aliasing={{}: (5, {})} | custom-call | tf_op jit(solution)/shard_map/invert/pallas_call | solution.py:192
  42.9 0.0 all-to-all-done
  42.9 5.2 %invert.4.refs_0_ = bf16[12,256,1024]{2,1,0:T(8,128)(2,1)} custom-call(s32[1]{0:T(128)} %bitcast.joined_ref, bf16[128,1536]{1,0:T(8,128)(2,1)S(1)} %bitcast.24, s32[1,1,256]{2,1,0:T(1,128)S(1)} %get-tuple-element.23.run_ref, bf16[2,128,1024]{2,1,0:T(8,128)(2,1)S(1)} %copy_multiply_fusion.back_ref, ...), custom_call_target="tpu_custom_call", output_to_operand_aliasing={{}: (5, {})} | custom-call | tf_op jit(solution)/shard_map/invert/pallas_call | solution.py:192
  48.2 0.0 collective-permute-done.1.refs_1_
  48.2 5.4 %invert.5 = bf16[12,256,1024]{2,1,0:T(8,128)(2,1)} custom-call(s32[1]{0:T(128)} %bitcast.joined_ref, bf16[128,1536]{1,0:T(8,128)(2,1)S(1)} %bitcast.25, s32[1,1,256]{2,1,0:T(1,128)S(1)} %get-tuple-element.24.run_ref, bf16[2,128,1024]{2,1,0:T(8,128)(2,1)S(1)} %copy_multiply_fusion.back_ref, ...), custom_call_target="tpu_custom_call", output_to_operand_aliasing={{}: (5, {})} | custom-call | tf_op jit(solution)/shard_map/invert/pallas_call | solution.py:192
  (8 shorter events, 0.2 us)
Async XLA Ops:
  1.4 10.8 %collective-permute-start = (bf16[1,128,512]{2,1,0:T(8,128)(2,1)S(1)}, bf16[1,128,512]{2,1,0:T(8,128)(2,1)S(1)}, u32[]{:S(2)}, u32[]{:S(2)}) collective-permute-start(bf16[1,128,512]{2,1,0:T(8,128)(2,1)S(1)} %pad_maximum_fusion.3), channel_id=1, source_target_pairs={{0,1},{1,2},{2,3},{3,4},{4,5},{5,6},{6,7},{7,8},{8,9},{9,10},{10,1... | collective-permute-start | bytes 393224 | tf_op jit(solution)/shard_map/ppermute | solution.py:224
  4.2 19.4 %all-to-all-start.1 = ((bf16[16,8,1536]{2,1,0:T(8,128)(2,1)}), bf16[16,8,1536]{2,1,0:T(8,128)(2,1)S(1)}, u32[]{:S(2)}, u32[]{:S(2)}) async-start(bf16[16,8,1536]{2,1,0:T(8,128)(2,1)} %bitcast.32), calls=%async_computation.1 | async-start | bytes 786432 | tf_op jit(solution)/shard_map/all_to_all | solution.py:253
  23.6 19.3 %all-to-all-start = ((bf16[16,8,1536]{2,1,0:T(8,128)(2,1)}), bf16[16,8,1536]{2,1,0:T(8,128)(2,1)S(1)}, u32[]{:S(2)}, u32[]{:S(2)}) async-start(bf16[16,8,1536]{2,1,0:T(8,128)(2,1)} %bitcast.31), calls=%async_computation | async-start | bytes 786432 | tf_op jit(solution)/shard_map/all_to_all | solution.py:254
  33.1 15.1 %collective-permute-start.1 = (bf16[256,1024]{1,0:T(8,128)(2,1)S(1)}, bf16[256,1024]{1,0:T(8,128)(2,1)S(1)}, u32[]{:S(2)}, u32[]{:S(2)}) collective-permute-start(bf16[256,1024]{1,0:T(8,128)(2,1)S(1)} %get-tuple-element.12), channel_id=1, source_target_pairs={{0,15},{1,0},{2,1},{3,2},{4,3},{5,4},{6,5},{7,6},{8,7},{9,8},{10,9... | collective-permute-start | bytes 1572872 | tf_op jit(solution)/shard_map/ppermute | solution.py:224

commit v6 on v5

--- a/solution.py
+++ b/solution.py
@@ -71,11 +71,12 @@
     return dot(jnp.concatenate([pick, pick], axis=0), both, ((0,), (0,)))
 
 
-def band_kernel(joined_ref, target_ref, run_ref, back_ref, ahead_ref, *refs, edge, base, held, late):
+def band_kernel(joined_ref, target_ref, run_ref, *refs, edge, base, held):
     refs = list(refs)
+    back_refs = [refs.pop(0) for _ in range(2 if edge else 1)]
+    ahead_refs = [refs.pop(0) for _ in range(2 if edge else 1)]
     if held:
         refs.pop(0)
-    late_ref = refs.pop(0) if late else None
     out_ref = refs.pop(0)
     above_ref = refs.pop(0) if edge else None
     target_sc, resid_sc, step_sc, energy_sc, factor_sc, image_sc, sem = refs
@@ -85,24 +86,21 @@
     elevations = factor_sc.shape[2]
     tile_width = energy_sc.shape[2]
     groups = -(-(columns // BAND + 2) // 16) * 16
-    weight_of = (0 if edge else 1,) + (1,) * (BAND - 1)
-    set_of = weight_of
+    weight_of = (0,) + (len(back_refs) - 1,) * (BAND - 1)
+    set_of = (0 if edge else 1,) + (1,) * (BAND - 1)
     span = [slice(q * columns, (q + 1) * columns) for q in range(BAND)]
 
     def copies(of):
         first = BAND * (base + of) - 1
         targets = [above_ref if edge and q == 0 else out_ref.at[first + q] for q in range(BAND)]
-        pairs = [pltpu.make_async_copy(image_sc.at[q], targets[q], sem.at[q]) for q in range(BAND)]
-        if late:
-            pairs.append(pltpu.make_async_copy(late_ref, out_ref.at[out_ref.shape[0] - 1], sem.at[BAND]))
-        return pairs
+        return [pltpu.make_async_copy(image_sc.at[q], targets[q], sem.at[q]) for q in range(BAND)]
 
     group = lax.broadcasted_iota(jnp.int32, (groups, columns), 0)
     picks = [
         jnp.where(group == run_ref[0, n : n + 1], 1.0, 0.0).astype(jnp.bfloat16)
         for n in range(run_ref.shape[1])
     ]
-    target_sc[...] = target_ref[...].astype(jnp.float32).T
+    target_sc[...] = target_ref[...].T
 
     def descend(is_first):
         for at in range(0, elevations, tile_width):
@@ -110,11 +108,11 @@
             imag = slice(elevations + at, elevations + at + tile_width)
             for q in range(BAND):
                 if is_first:
-                    resid = target_sc[span[q]].astype(jnp.bfloat16)
+                    resid = target_sc[span[q]]
                 else:
                     resid = resid_sc[span[q]]
-                step_real = dot(resid, back_ref[weight_of[q], :, real])
-                step_imag = dot(resid, back_ref[weight_of[q], :, imag])
+                step_real = dot(resid, back_refs[weight_of[q]][:, real])
+                step_imag = dot(resid, back_refs[weight_of[q]][:, imag])
                 if not is_first:
                     factor = factor_sc[set_of[q], :, real]
                     step_real += step_sc[span[q], real] * factor
@@ -146,8 +144,10 @@
             for half in range(2):
                 part = slice(half * elevations, (half + 1) * elevations)
                 rounded = (step_sc[span[q], part] * factor_sc[set_of[q]]).astype(jnp.bfloat16)
-                guess += dot(rounded, ahead_ref[weight_of[q], part])
-            resid_sc[span[q]] = (target_sc[span[q]] - guess).astype(jnp.bfloat16)
+                guess += dot(rounded, ahead_refs[weight_of[q]][part])
+            resid_sc[span[q]] = (target_sc[span[q]].astype(jnp.float32) - guess).astype(
+                jnp.bfloat16
+            )
 
     descend(True)
 
@@ -158,7 +158,7 @@
 
     @pl.when(step > 0)
     def _():
-        for copy in copies(step - 1)[:BAND]:
+        for copy in copies(step - 1):
             copy.wait()
 
     for q in range(BAND):
@@ -171,52 +171,67 @@
 
     @pl.when(step == steps - 1)
     def _():
-        if late:
-            copies(step)[BAND].start()
         for copy in copies(step):
             copy.wait()
 
 
-def invert(joined, targets, runs, back, ahead, out_shape, *, offset, base, edge=False, out=None, late=None):
+def invert(joined, targets, runs, backs, aheads, out_shape, *, offset, base, edge=False, out=None):
     lines = targets.shape[0]
     steps, kinds, columns = runs.shape
-    elevations = back.shape[2] // 2
+    elevations = backs[0].shape[1] // 2
     whole = pl.BlockSpec(memory_space=pltpu.VMEM)
     far = pl.BlockSpec(memory_space=pl.ANY)
     pixels = BAND * columns
     tile_width = 256
     shape = jax.ShapeDtypeStruct(out_shape, jnp.bfloat16)
     above = jax.ShapeDtypeStruct(out_shape[1:], jnp.bfloat16)
-    extra = ([] if out is None else [out]) + ([] if late is None else [late])
-    extra_specs = ([] if out is None else [far]) + ([] if late is None else [whole])
+    weights = [*backs, *aheads]
+    extra = [] if out is None else [out]
     return pl.pallas_call(
-        functools.partial(
-            band_kernel, edge=edge, base=base, held=out is not None, late=late is not None
-        ),
+        functools.partial(band_kernel, edge=edge, base=base, held=out is not None),
         grid=(steps,),
         in_specs=[
             pl.BlockSpec(memory_space=pltpu.SMEM),
             pl.BlockSpec((lines, pixels), lambda i: (0, i + offset)),
             pl.BlockSpec((1, kinds, columns), lambda i: (i, 0, 0)),
-            whole,
-            whole,
         ]
-        + extra_specs,
+        + [whole] * len(weights)
+        + [far] * len(extra),
         out_specs=[far, far] if edge else far,
         out_shape=[shape, above] if edge else shape,
-        input_output_aliases={} if out is None else {5: 0},
+        input_output_aliases={} if out is None else {3 + len(weights): 0},
         scratch_shapes=[
-            pltpu.VMEM((pixels, lines), jnp.float32),
+            pltpu.VMEM((pixels, lines), jnp.bfloat16),
             pltpu.VMEM((pixels, lines), jnp.bfloat16),
             pltpu.VMEM((pixels, 2 * elevations), jnp.float32),
             pltpu.VMEM((2 * (elevations // tile_width), columns, tile_width), jnp.float32),
             pltpu.VMEM((2, columns, elevations), jnp.float32),
             pltpu.VMEM((BAND, columns, 2 * elevations), jnp.bfloat16),
-            pltpu.SemaphoreType.DMA((BAND + 1,)),
+            pltpu.SemaphoreType.DMA((BAND,)),
         ],
         compiler_params=pltpu.CompilerParams(vmem_limit_bytes=40 * 1024 * 1024),
         name="invert_edge" if edge else "invert",
-    )(joined, targets, runs, back, ahead, *extra)
+    )(joined, targets, runs, *weights, *extra)
+
+
+def place_kernel(row_ref, _, out_ref, sem):
+    copy = pltpu.make_async_copy(row_ref, out_ref.at[out_ref.shape[0] - 1], sem)
+    copy.start()
+    copy.wait()
+
+
+def place_last_row(row, out):
+    far = pl.BlockSpec(memory_space=pl.ANY)
+    return pl.pallas_call(
+        place_kernel,
+        in_specs=[pl.BlockSpec(memory_space=pltpu.VMEM), far],
+        out_specs=far,
+        out_shape=jax.ShapeDtypeStruct(out.shape, out.dtype),
+        input_output_aliases={1: 0},
+        scratch_shapes=[pltpu.SemaphoreType.DMA],
+        compiler_params=pltpu.CompilerParams(vmem_limit_bytes=4 * 1024 * 1024),
+        name="place_last_row",
+    )(row, out)
 
 
 def turned(value, step):
@@ -232,11 +247,12 @@
 
 
 def planes_of(steering, acqs):
-    count, lines, elevations = steering.shape
-    real, imag = steering[:, : lines // 2], steering[:, lines // 2 :]
-    upper = jnp.concatenate([real, -imag], axis=2).reshape(count, -1, 1, acqs, 2 * elevations)
-    lower = jnp.concatenate([imag, real], axis=2).reshape(count, -1, 1, acqs, 2 * elevations)
-    return jnp.concatenate([upper, lower], axis=2).reshape(count, lines, 2 * elevations)
+    _, lines, elevations = steering.shape
+    real, imag = steering[0, : lines // 2], steering[0, lines // 2 :]
+    upper = jnp.concatenate([real, -imag], axis=1).reshape(-1, 1, acqs, 2 * elevations)
+    lower = jnp.concatenate([imag, real], axis=1).reshape(-1, 1, acqs, 2 * elevations)
+    plane = jnp.concatenate([upper, lower], axis=1).reshape(lines, 2 * elevations)
+    return plane * STEP_SIZE, plane.T
 
 
 def program(measurements, tile_order, steer_phase, group_ids):
@@ -254,9 +270,8 @@
     tail = lax.all_to_all(sent[1], "acq", 0, 0, tiled=True)
     mine = steering_of(steer_phase)
     before = turned(mine, 1)
-    back = planes_of(jnp.concatenate([before, mine], axis=0), acqs)
-    ahead = back.transpose(0, 2, 1)
-    back = back * STEP_SIZE
+    back, ahead = planes_of(mine, acqs)
+    back_before, ahead_before = planes_of(before, acqs)
     runs = (group_ids % columns + BAND - 1) // BAND
     first = lax.axis_index("acq") == 0
     column = jnp.arange(columns, dtype=jnp.int32)
@@ -267,17 +282,19 @@
     inner_runs = runs[BAND - 1 : rows - 1 : BAND][:, None]
     joined = jnp.where(first, 0, 1).reshape(1)
     shape = (rows, columns, 2 * elevations)
-    out, above = invert(joined, head, edge_runs, back, ahead, shape, offset=0, base=0, edge=True)
+    out = invert(
+        joined, head, inner_runs[:early], [back], [ahead], shape, offset=1, base=1
+    )
+    out, above = invert(
+        joined, head, edge_runs, [back_before, back], [ahead_before, ahead], shape,
+        offset=0, base=0, edge=True, out=out,
+    )
     late = turned(above, -1)
-    out = invert(joined, head, inner_runs[:early], back, ahead, shape, offset=1, base=1, out=out)
     out = invert(
-        joined, tail, inner_runs[early:-1], back, ahead, shape,
+        joined, tail, inner_runs[early:], [back], [ahead], shape,
         offset=0, base=1 + early, out=out,
     )
-    return invert(
-        joined, tail, inner_runs[-1:], back, ahead, shape,
-        offset=bands - 2 - early, base=bands - 1, out=out, late=late,
-    )
+    return place_last_row(late, out)
 
 
 def solution(mesh):

time: 54.1 us -> 52.7 us (0.974)
  Pallas kernels: 23.9 us -> 23 us
  waiting for transfers between devices: 9.42 us -> 10.3 us
  other arithmetic: 3.12 us -> 2.56 us
    pallas_call x4 -> x3, Pallas kernels: 21.6 us -> 19.9 us  [invert(): pl.pallas_call(functools.partial(band_kernel, edge=edge, base=base, held=...]
    all_to_all x1, waiting for transfers between devices: 9.42 us -> 10.3 us  [program(): head = lax.all_to_all(sent[0], 'acq', 0, 0, tiled=True)]
    pallas_call x0 -> x1, Pallas kernels: none -> 0.81 us  [place_last_row(): pl.pallas_call(place_kernel, in_specs=[pl.BlockSpec(memory_space=pltpu.VM...]
    reshape x3 -> x4, local copies, waits for them, and re-layouts: 1.11 us -> 0.47 us  [planes_of(): jnp.concatenate([upper, lower], axis=1).reshape(lines, 2 * elevations)]
  transfers between devices with their start and end apart: 4 -> 4, of which waited for: 1 -> 1; matrix products, arithmetic and copies ran while one was open for 5% -> 3% of each run, Pallas kernels for 34% -> 42%
where the time goes in v6:
time: 52.7 us; the launch traced here: 52.3 us
  Pallas kernels  23 us (44%)
  starting transfers between devices  15.7 us (30%)
  waiting for transfers between devices  10.3 us (20%)
  other arithmetic  2.56 us (5%)
  local copies, waits for them, and re-layouts  0.6 us (1%)
    pallas_call x3, Pallas kernels, invert(): pl.pallas_call(functools.partial(band_kernel, edge=edge, base=base, held=...  19.9 us
    all_to_all x1, waiting for transfers between devices, program(): head = lax.all_to_all(sent[0], 'acq', 0, 0, tiled=True)  10.3 us
    all_to_all x1, starting transfers between devices, program(): head = lax.all_to_all(sent[0], 'acq', 0, 0, tiled=True)  7.21 us
    ppermute x2, starting transfers between devices, turned(): lax.ppermute(value, 'acq', [(i, (i + step) % count) for i in range(count)])  4.91 us
    all_to_all x1, starting transfers between devices, program(): tail = lax.all_to_all(sent[1], 'acq', 0, 0, tiled=True)  3.55 us
    pallas_call x1, Pallas kernels, order_tiles(): pl.pallas_call(functools.partial(order_kernel, spans=spans, ahead_rows=ah...  2.27 us
    convert_element_type x1, other arithmetic, steering_of(): real = (jnp.cos(phase) * scale).astype(jnp.bfloat16)  1.37 us
  transfers between devices with their start and end apart: 4, of which 1 were waited for; matrix products, arithmetic and copies ran while one was open for 3% of the time, Pallas kernels for 42%

profile of v6, /device:TPU:0, one launch (start us, length us, event | category | flops | bytes accessed | tf_op | source)
XLA Modules:
  0.0 52.3 jit_solution(18223829952542204083)
XLA Ops:
  0.0 1.4 %multiply_convert_fusion.1 = (bf16[1,64,512]{2,1,0:T(8,128)(2,1)S(1)}, bf16[1,64,512]{2,1,0:T(8,128)(2,1)S(1)}) fusion(f32[1,64,512]{2,1,0:T(8,128)} %param.6), kind=kLoop, calls=%fused_computation.6 | loop fusion | flops 131072 | bytes 262144 | tf_op jit(solution)/shard_map/convert_element_type | solution.py:244
  1.4 0.5 %collective-permute-start = (bf16[1,128,512]{2,1,0:T(8,128)(2,1)S(1)}, bf16[1,128,512]{2,1,0:T(8,128)(2,1)S(1)}, u32[]{:S(2)}, u32[]{:S(2)}) collective-permute-start(bf16[1,128,512]{2,1,0:T(8,128)(2,1)S(1)} %pad_maximum_fusion), channel_id=1, source_target_pairs={{0,1},{1,2},{2,3},{3,4},{4,5},{5,6},{6,7},{7,8},{8,9},{9,10},{10,1... | collective-permute-start | bytes 393224 | tf_op jit(solution)/shard_map/ppermute | solution.py:239
  1.9 2.3 %order_tiles.1 = (bf16[128,1536]{1,0:T(8,128)(2,1)}, bf16[128,1536]{1,0:T(8,128)(2,1)}) custom-call(s32[16]{0:T(128)} %order_ref.1, bf16[4,2,12,16,256]{4,3,2,1,0:T(8,128)(2,1)} %bitcast.25), custom_call_target="tpu_custom_call" | custom-call | tf_op jit(solution)/shard_map/order_tiles/pallas_call | solution.py:51
  4.2 7.2 %all-to-all-start = ((bf16[16,8,1536]{2,1,0:T(8,128)(2,1)}), bf16[16,8,1536]{2,1,0:T(8,128)(2,1)S(1)}, u32[]{:S(2)}, u32[]{:S(2)}) async-start(bf16[16,8,1536]{2,1,0:T(8,128)(2,1)} %bitcast.29), calls=%async_computation | async-start | bytes 786432 | tf_op jit(solution)/shard_map/all_to_all | solution.py:269
  11.5 0.7 %add_select_fusion = s32[12,256]{1,0:T(8,128)S(1)} fusion(s32[12,256]{1,0:T(8,128)} %param.7), kind=kLoop, calls=%fused_computation.7 | loop fusion | flops 61440 | bytes 24576 | tf_op jit(solution)/shard_map/jit(floor_divide)/jit(_where)/select_n | solution.py:275
  12.3 0.1 maximum_maximum_fusion.1
  12.5 0.1 reshape.125
  12.6 0.2 copy.29
  12.8 0.0 collective-permute-done
  12.9 0.1 maximum_maximum_fusion
  13.0 0.1 reshape.124
  13.1 0.2 copy.28
  13.3 10.3 %all-to-all-done = bf16[16,8,1536]{2,1,0:T(8,128)(2,1)S(1)} async-done(((bf16[16,8,1536]{2,1,0:T(8,128)(2,1)}), bf16[16,8,1536]{2,1,0:T(8,128)(2,1)S(1)}, u32[]{:S(2)}, u32[]{:S(2)}) %all-to-all-start) | async-done | bytes 393248 | tf_op jit(solution)/shard_map/all_to_all | solution.py:269
  23.6 3.6 %all-to-all-start.1 = ((bf16[16,8,1536]{2,1,0:T(8,128)(2,1)}), bf16[16,8,1536]{2,1,0:T(8,128)(2,1)S(1)}, u32[]{:S(2)}, u32[]{:S(2)}) async-start(bf16[16,8,1536]{2,1,0:T(8,128)(2,1)} %bitcast.28), calls=%async_computation.1 | async-start | bytes 786432 | tf_op jit(solution)/shard_map/all_to_all | solution.py:270
  27.2 5.1 %invert.2.refs_4_ = bf16[12,256,1024]{2,1,0:T(8,128)(2,1)} custom-call(s32[1]{0:T(128)} %bitcast.joined_ref, bf16[128,1536]{1,0:T(8,128)(2,1)S(1)} %bitcast.21, s32[1,1,256]{2,1,0:T(1,128)S(1)} %slice_bitcast_fusion.run_ref, bf16[128,1024]{1,0:T(8,128)(2,1)S(1)} %broadcast_multiply_fusion.refs_0_.refs_1_, bf16[1024,128]{1,0:T(8,128)(2,1)S(1)} %bitcast.18), custom_call_target="tpu_custom_call" | custom-call | tf_op jit(solution)/shard_map/invert/pallas_call | solution.py:190
  32.3 5.6 %invert_edge.1 = (bf16[12,256,1024]{2,1,0:T(8,128)(2,1)}, bf16[256,1024]{1,0:T(8,128)(2,1)S(1)}) custom-call(s32[1]{0:T(128)} %bitcast.joined_ref, bf16[128,1536]{1,0:T(8,128)(2,1)S(1)} %bitcast.22, s32[1,2,256]{2,1,0:T(2,128)S(1)} %add_bitcast_fusion.run_ref, ...), custom_call_target="tpu_custom_call", output_to_operand_aliasing={{0}: (7, {})} | custom-call | tf_op jit(solution)/shard_map/invert_edge/pallas_call | solution.py:190
  37.9 4.4 %collective-permute-start.1 = (bf16[256,1024]{1,0:T(8,128)(2,1)S(1)}, bf16[256,1024]{1,0:T(8,128)(2,1)S(1)}, u32[]{:S(2)}, u32[]{:S(2)}) collective-permute-start(bf16[256,1024]{1,0:T(8,128)(2,1)S(1)} %get-tuple-element.10), channel_id=1, source_target_pairs={{0,15},{1,0},{2,1},{3,2},{4,3},{5,4},{6,5},{7,6},{8,7},{9,8},{10,9... | collective-permute-start | bytes 1572872 | tf_op jit(solution)/shard_map/ppermute | solution.py:239
  42.3 0.0 all-to-all-done.1
  42.3 9.2 %invert.3._ = bf16[12,256,1024]{2,1,0:T(8,128)(2,1)} custom-call(s32[1]{0:T(128)} %bitcast.joined_ref, bf16[128,1536]{1,0:T(8,128)(2,1)S(1)} %bitcast.23, s32[2,1,256]{2,1,0:T(1,128)S(1)} %slice.32.run_ref, bf16[128,1024]{1,0:T(8,128)(2,1)S(1)} %broadcast_multiply_fusion.refs_0_.refs_1_, ...), custom_call_target="tpu_custom_call", output_to_operand_aliasing={{}: (5, {})} | custom-call | tf_op jit(solution)/shard_map/invert/pallas_call | solution.py:190
  51.5 0.0 collective-permute-done.1.row_ref
  51.5 0.8 %place_last_row.1 = bf16[12,256,1024]{2,1,0:T(8,128)(2,1)} custom-call(bf16[256,1024]{1,0:T(8,128)(2,1)S(1)} %collective-permute-done.1.row_ref, bf16[12,256,1024]{2,1,0:T(8,128)(2,1)} %invert.3._), custom_call_target="tpu_custom_call", output_to_operand_aliasing={{}: (1, {})} | custom-call | tf_op jit(solution)/shard_map/place_last_row/pallas_call | solution.py:225
  (16 shorter events, 0.3 us)
Async XLA Ops:
  1.4 11.4 %collective-permute-start = (bf16[1,128,512]{2,1,0:T(8,128)(2,1)S(1)}, bf16[1,128,512]{2,1,0:T(8,128)(2,1)S(1)}, u32[]{:S(2)}, u32[]{:S(2)}) collective-permute-start(bf16[1,128,512]{2,1,0:T(8,128)(2,1)S(1)} %pad_maximum_fusion), channel_id=1, source_target_pairs={{0,1},{1,2},{2,3},{3,4},{4,5},{5,6},{6,7},{7,8},{8,9},{9,10},{10,1... | collective-permute-start | bytes 393224 | tf_op jit(solution)/shard_map/ppermute | solution.py:239
  4.2 19.4 %all-to-all-start = ((bf16[16,8,1536]{2,1,0:T(8,128)(2,1)}), bf16[16,8,1536]{2,1,0:T(8,128)(2,1)S(1)}, u32[]{:S(2)}, u32[]{:S(2)}) async-start(bf16[16,8,1536]{2,1,0:T(8,128)(2,1)} %bitcast.29), calls=%async_computation | async-start | bytes 786432 | tf_op jit(solution)/shard_map/all_to_all | solution.py:269
  23.6 18.7 %all-to-all-start.1 = ((bf16[16,8,1536]{2,1,0:T(8,128)(2,1)}), bf16[16,8,1536]{2,1,0:T(8,128)(2,1)S(1)}, u32[]{:S(2)}, u32[]{:S(2)}) async-start(bf16[16,8,1536]{2,1,0:T(8,128)(2,1)} %bitcast.28), calls=%async_computation.1 | async-start | bytes 786432 | tf_op jit(solution)/shard_map/all_to_all | solution.py:270
  37.9 13.6 %collective-permute-start.1 = (bf16[256,1024]{1,0:T(8,128)(2,1)S(1)}, bf16[256,1024]{1,0:T(8,128)(2,1)S(1)}, u32[]{:S(2)}, u32[]{:S(2)}) collective-permute-start(bf16[256,1024]{1,0:T(8,128)(2,1)S(1)} %get-tuple-element.10), channel_id=1, source_target_pairs={{0,15},{1,0},{2,1},{3,2},{4,3},{5,4},{6,5},{7,6},{8,7},{9,8},{10,9... | collective-permute-start | bytes 1572872 | tf_op jit(solution)/shard_map/ppermute | solution.py:239
